TPU v7x, 128 devices: a whole 4x4x4 slice. The times are simulated.
128 devices in a mesh: req: 64 (over z_lo, x, y, core), kvh: 2 (over z_hi).
Axes of the slice: x: 4, y: 4, z: 4 (z_hi: 2, z_lo: 2; z = z_hi * 2 + z_lo), core: 2. Of those that a mesh axis runs over, the one named last changes fastest.
Arguments:
- queries: bfloat16 [64, 4, 8192], P('req', None, 'kvh'), may hold values from -42 to 42
- incoming_keys: bfloat16 [64, 4, 1024], P('req', None, 'kvh'), may hold values from -6 to 6
- incoming_values: bfloat16 [64, 4, 1024], P('req', None, 'kvh'), may hold values from -6 to 6
- system_prefix_keys: bfloat16 [8, 16384, 1024], P(None, 'req', 'kvh'), may hold values from -6 to 6
- system_prefix_values: bfloat16 [8, 16384, 1024], P(None, 'req', 'kvh'), may hold values from -6 to 6
- request_history_keys: bfloat16 [64, 2048, 1024], P('req', None, 'kvh'), may hold values from -6 to 6
- request_history_values: bfloat16 [64, 2048, 1024], P('req', None, 'kvh'), may hold values from -6 to 6
- kept: int32 [64, 8, 1024], P('req', 'kvh'), may hold values from 0 to 2047, as said below
- membership: int32 [64, 1], P('req'), may hold values from 0 to 7; in each aligned block of 64 rows (0 to 63, 64 to 127, ...) at most 16 rows name the same one
- out_weight: bfloat16 [8192, 8192], P('kvh', 'req'), may hold values from -0.0625 to 0.0625
Outputs:
- layer_out: bfloat16 [64, 4, 8192], P(None, None, 'req')
Inputs may be any that keep to these rules, and one draw needn't show every extreme that they name: `membership`: no system prompt has more than 16 requests; some prompt has exactly 16. `kept`: the 1024 positions of one request and KV head are distinct.
All inputs are finite; a program needn't handle non-finite values.
Results may differ from a plain program's by a relative error of at most 0.0049.
Values may be sent and summed in bfloat16 or wider, within the bound.
No kernel may reach another device: no remote copies, remote signals or barrier semaphores. Data moves between devices by JAX's collectives and lax.ppermute only.
A program may use at most 128 MiB of HBM per device.

v0:
```python
import jax
import jax.numpy as jnp
from jax import lax
from jax.sharding import PartitionSpec as P

HEAD_WIDTH = 128
HEADS_PER_GROUP = 8
PROMPT_COUNT = 8


def local_partial(scores):
    row_peak = jnp.max(scores, axis=-1)
    exp_terms = jnp.exp(scores - row_peak[..., None])
    row_total = jnp.sum(exp_terms, axis=-1)
    return (row_peak, row_total, exp_terms.astype(jnp.bfloat16))


def prefix_partials(
    query_all, member_all, system_prefix_keys, system_prefix_values, kv_local, score_scale
):
    total_rows, span_steps = (query_all.shape[0], query_all.shape[1])
    capacity = total_rows // 4
    stretch_len = system_prefix_keys.shape[1]
    member_ids = member_all[:, 0]
    onehot_table = member_ids[:, None] == jnp.arange(PROMPT_COUNT)[None, :]
    prompt_counts = jnp.sum(onehot_table.astype(jnp.int32), axis=0)
    prompt_starts = jnp.cumsum(prompt_counts) - prompt_counts
    sorted_order = jnp.argsort(member_ids, stable=True)
    grouped_query_heads = query_all.reshape(
        total_rows, span_steps, kv_local, HEADS_PER_GROUP, HEAD_WIDTH
    )
    peak_all = jnp.zeros((total_rows, span_steps, kv_local, HEADS_PER_GROUP), jnp.float32)
    total_all = jnp.zeros((total_rows, span_steps, kv_local, HEADS_PER_GROUP), jnp.float32)
    out_all = jnp.zeros(
        (total_rows, span_steps, kv_local, HEADS_PER_GROUP, HEAD_WIDTH), jnp.float32
    )
    slot_ids = jnp.arange(capacity)
    for prompt_id in range(PROMPT_COUNT):
        slot_pos = jnp.minimum(prompt_starts[prompt_id] + slot_ids, total_rows - 1)
        slot_rows = sorted_order[slot_pos]
        is_valid = (slot_ids < prompt_counts[prompt_id])[:, None, None, None]
        chosen_index = grouped_query_heads[slot_rows]
        stretch_keys = system_prefix_keys[prompt_id].reshape(stretch_len, kv_local, HEAD_WIDTH)
        stretch_values = system_prefix_values[prompt_id].reshape(stretch_len, kv_local, HEAD_WIDTH)
        scores = (
            jnp.einsum(
                "cskgd,lkd->cskgl", chosen_index, stretch_keys, preferred_element_type=jnp.float32
            )
            * score_scale
        )
        row_peak, row_total, weights = local_partial(scores)
        part_out = jnp.einsum(
            "cskgl,lkd->cskgd", weights, stretch_values, preferred_element_type=jnp.float32
        )
        peak_all = peak_all.at[slot_rows].add(jnp.where(is_valid, row_peak, 0.0))
        total_all = total_all.at[slot_rows].add(jnp.where(is_valid, row_total, 0.0))
        out_all = out_all.at[slot_rows].add(jnp.where(is_valid[..., None], part_out, 0.0))
    return (peak_all, total_all, out_all)


def return_partials(peak_all, total_all, out_all, req_rows):
    total_rows, span_steps, kv_local = (peak_all.shape[0], peak_all.shape[1], peak_all.shape[2])
    flat_peak = peak_all.reshape(total_rows, span_steps, kv_local * HEADS_PER_GROUP)
    flat_total = total_all.reshape(total_rows, span_steps, kv_local * HEADS_PER_GROUP)
    flat_out = out_all.reshape(total_rows, span_steps, kv_local * HEADS_PER_GROUP * HEAD_WIDTH)
    got_out, got_peak, got_total = (
        lax.all_to_all(flat_out, "req", split_axis=0, concat_axis=0, tiled=True),
        lax.all_to_all(flat_peak, "req", split_axis=0, concat_axis=0, tiled=True),
        lax.all_to_all(flat_total, "req", split_axis=0, concat_axis=0, tiled=True),
    )
    sources = total_rows // req_rows
    return (
        got_peak.reshape(sources, req_rows, span_steps, kv_local, HEADS_PER_GROUP),
        got_total.reshape(sources, req_rows, span_steps, kv_local, HEADS_PER_GROUP),
        got_out.reshape(sources, req_rows, span_steps, kv_local, HEADS_PER_GROUP, HEAD_WIDTH),
    )


def local(
    queries,
    incoming_keys,
    incoming_values,
    system_prefix_keys,
    system_prefix_values,
    request_history_keys,
    request_history_values,
    kept,
    membership,
    out_weight,
):
    req_rows, step_count, query_width = queries.shape
    kv_local = incoming_keys.shape[2] // HEAD_WIDTH
    score_scale = HEAD_WIDTH ** (-0.5)
    grouped_query_heads = queries.reshape(
        req_rows, step_count, kv_local, HEADS_PER_GROUP, HEAD_WIDTH
    )
    cache_keys = request_history_keys.reshape(req_rows, -1, kv_local, HEAD_WIDTH)
    cache_values = request_history_values.reshape(req_rows, -1, kv_local, HEAD_WIDTH)
    head_index_list = jnp.arange(kv_local)[None, :]
    retained_keys = jax.vmap(lambda key_table, pick_list: key_table[pick_list.T, head_index_list])(
        cache_keys, kept
    )
    retained_values = jax.vmap(
        lambda value_table, pick_list: value_table[pick_list.T, head_index_list]
    )(cache_values, kept)
    kept_scores = (
        jnp.einsum(
            "rtkgd,rlkd->rtkgl",
            grouped_query_heads,
            retained_keys,
            preferred_element_type=jnp.float32,
        )
        * score_scale
    )
    kept_peak, kept_total, kept_weights = local_partial(kept_scores)
    kept_out = jnp.einsum(
        "rtkgl,rlkd->rtkgd", kept_weights, retained_values, preferred_element_type=jnp.float32
    )
    recent_token_keys = incoming_keys.reshape(req_rows, step_count, kv_local, HEAD_WIDTH)
    recent_token_values = incoming_values.reshape(req_rows, step_count, kv_local, HEAD_WIDTH)
    fresh_scores = (
        jnp.einsum(
            "rtkgd,rukd->rtkgu",
            grouped_query_heads,
            recent_token_keys,
            preferred_element_type=jnp.float32,
        )
        * score_scale
    )
    causal_mask = jnp.arange(step_count)[None, :] <= jnp.arange(step_count)[:, None]
    fresh_scores = jnp.where(causal_mask[None, :, None, None, :], fresh_scores, -1e30)
    recent_score_peak, recent_weight_sum, fresh_weights = local_partial(fresh_scores)
    recent_output = jnp.einsum(
        "rtkgu,rukd->rtkgd", fresh_weights, recent_token_values, preferred_element_type=jnp.float32
    )
    partial_sets = []
    for step_index in range(step_count):
        query_all, member_all = (
            lax.all_gather(queries[:, step_index : step_index + 1], "req", axis=0, tiled=True),
            lax.all_gather(membership, "req", axis=0, tiled=True),
        )
        partial_sets.append(
            return_partials(
                *prefix_partials(
                    query_all,
                    member_all,
                    system_prefix_keys,
                    system_prefix_values,
                    kv_local,
                    score_scale,
                ),
                req_rows
            )
        )
    src_peak = jnp.concatenate([entry[0] for entry in partial_sets], axis=2)
    src_total = jnp.concatenate([entry[1] for entry in partial_sets], axis=2)
    src_out = jnp.concatenate([entry[2] for entry in partial_sets], axis=2)
    top_score = jnp.maximum(jnp.maximum(jnp.max(src_peak, axis=0), kept_peak), recent_score_peak)
    src_factor = jnp.exp(src_peak - top_score[None])
    kept_factor = jnp.exp(kept_peak - top_score)
    fresh_factor = jnp.exp(recent_score_peak - top_score)
    numerator = (
        jnp.sum(src_factor[..., None] * src_out, axis=0)
        + kept_factor[..., None] * kept_out
        + fresh_factor[..., None] * recent_output
    )
    denominator = (
        jnp.sum(src_factor * src_total, axis=0)
        + kept_factor * kept_total
        + fresh_factor * recent_weight_sum
    )
    attention = (
        (numerator / denominator[..., None])
        .astype(jnp.bfloat16)
        .reshape(req_rows, step_count, query_width)
    )
    piece_rows = lax.all_gather(attention, "req", axis=0, tiled=True)
    flat_rows = piece_rows.reshape(-1, query_width)
    partial_out = jnp.dot(flat_rows, out_weight, preferred_element_type=jnp.float32).reshape(
        piece_rows.shape[0], step_count, -1
    )
    return lax.psum(partial_out, "kvh").astype(jnp.bfloat16)


def solution(mesh):
    placed = (
        P("req", None, "kvh"),
        P("req", None, "kvh"),
        P("req", None, "kvh"),
        P(None, "req", "kvh"),
        P(None, "req", "kvh"),
        P("req", None, "kvh"),
        P("req", None, "kvh"),
        P("req", "kvh", None),
        P("req", None),
        P("kvh", "req"),
    )
    return jax.shard_map(
        local, mesh=mesh, in_specs=placed, out_specs=P(None, None, "req"), check_vma=False
    )
```

profile of v0, /device:TPU:1, one launch (start us, length us, event | category | flops | bytes accessed | tf_op | source)
XLA Modules:
  0.0 1134.3 jit_solution(11656335214572381754)
XLA Ops:
  9.2 17.4 %all-reduce = s32[64]{0:T(128)S(1)} all-reduce(s32[64]{0:T(128)S(1)} %bitcast_dynamic-update-slice_fusion), channel_id=1, replica_groups=mesh['req'=64,'kvh'=2] {'req'}, use_global_device_ids=true, to_apply=%add | all-reduce | flops 64 | bytes 512 | tf_op jit(solution)/shard_map/squeeze | solution.py:24
  32.7 83.6 %all_gather.22 = bf16[64,1,4096]{2,1,0:T(2,128)(2,1)S(1)} all-gather(bf16[1,1,4096]{2,1,0:T(2,128)(2,1)S(1)} %get-tuple-element.26), channel_id=1, replica_groups=mesh['req'=64,'kvh'=2] {'req'}, dimensions={0}, use_global_device_ids=true | all-gather | bytes 532480 | tf_op jit(solution)/shard_map/all_gather | solution.py:139
  116.2 3.3 reduce.71
  119.6 80.7 %all_gather.23 = bf16[64,1,4096]{2,1,0:T(2,128)(2,1)S(1)} all-gather(bf16[1,1,4096]{2,1,0:T(2,128)(2,1)S(1)} %get-tuple-element.28), channel_id=1, replica_groups=mesh['req'=64,'kvh'=2] {'req'}, dimensions={0}, use_global_device_ids=true | all-gather | bytes 532480 | tf_op jit(solution)/shard_map/all_gather | solution.py:139
  200.3 3.3 reduce.72
  209.2 90.7 %all_gather.24 = bf16[64,1,4096]{2,1,0:T(2,128)(2,1)S(1)} all-gather(bf16[1,1,4096]{2,1,0:T(2,128)(2,1)S(1)} %get-tuple-element.27), channel_id=1, replica_groups=mesh['req'=64,'kvh'=2] {'req'}, dimensions={0}, use_global_device_ids=true | all-gather | bytes 532480 | tf_op jit(solution)/shard_map/all_gather | solution.py:139
  299.9 4.1 reduce.73
  307.6 85.8 %all_gather.25 = bf16[64,1,4096]{2,1,0:T(2,128)(2,1)} all-gather(bf16[1,1,4096]{2,1,0:T(2,128)(2,1)S(1)} %get-tuple-element.29), channel_id=1, replica_groups=mesh['req'=64,'kvh'=2] {'req'}, dimensions={0}, use_global_device_ids=true | all-gather | bytes 532480 | tf_op jit(solution)/shard_map/all_gather | solution.py:139
  393.3 5.1 reduce.74
  438.6 2.7 fusion.409
  515.0 5.1 all-to-all-start.11
  520.2 2.9 fusion.408
  565.2 9.7 all-to-all-start.10
  597.3 9.1 all-to-all-start.9
  625.1 9.8 all-to-all-start.8
  652.8 9.1 all-to-all-start.3
  680.6 9.6 all-to-all-start.2
  703.0 8.9 all-to-all-start.1
  725.5 9.2 all-to-all-start
  757.7 2.5 scatter_fusion.63
  760.2 9.7 all-to-all-start.7
  799.0 9.9 all-to-all-start.6
  835.3 9.5 all-to-all-start.5
  845.8 4.0 reshape.1933
  855.1 66.4 %gather_fusion.40 = bf16[4096,128]{1,0:T(8,128)(2,1)} fusion(bf16[1,2048,4,128]{3,2,1,0:T(4,128)(2,1)} %reshape.1933, s32[4096]{0:T(1024)S(1)} %reshape.2369), kind=kCustom, calls=%fused_computation.40 | custom fusion | bytes 2146304 | tf_op jit(solution)/shard_map/vmap()/gather | solution.py:100
  943.9 9.0 all-to-all-start.4
  953.2 2.6 reshape.1973
  955.8 40.2 %gather_fusion.41 = bf16[4096,128]{1,0:T(8,128)(2,1)} fusion(bf16[1,2048,4,128]{3,2,1,0:T(4,128)(2,1)S(1)} %reshape.1973, s32[4096]{0:T(1024)S(1)} %reshape.2369), kind=kCustom, calls=%fused_computation.41 | custom fusion | bytes 2146304 | tf_op jit(solution)/shard_map/vmap()/gather | solution.py:104
  1002.0 3.6 fusion
  1006.7 105.1 %all-gather.2.cloned.1.call-done = bf16[64,4,4096]{2,1,0:T(4,128)(2,1)} async-done(((bf16[1,4,4096]{2,1,0:T(4,128)(2,1)}), bf16[64,4,4096]{2,1,0:T(4,128)(2,1)}) %all-gather.2.cloned.1.call-update) | async-done | bytes 2097168 | tf_op jit(solution)/shard_map/all_gather | solution.py:177
  1111.8 4.1 fusion.1
  1115.9 10.6 all-reduce.2
  (954 shorter events, 387.9 us)
Async XLA Ops:
  6.5 1105.3 %copy-start = (bf16[4096,128]{1,0:T(8,128)(2,1)S(1)}, bf16[4096,128]{1,0:T(8,128)(2,1)}, u32[]{:S(2)}) copy-start(bf16[4096,128]{1,0:T(8,128)(2,1)} %param.19) | copy-start | bytes 3145732
  515.0 50.2 %all-to-all-start.11 = ((f32[64,1,32]{2,1,0:T(1,128)}), f32[64,1,32]{2,1,0:T(1,128)}, u32[]{:S(2)}, u32[]{:S(2)}) async-start(f32[64,1,32]{2,1,0:T(1,128)} %copy.1020), calls=%async_computation.11 | async-start | bytes 65536 | tf_op jit(solution)/shard_map/all_to_all | solution.py:69
  556.2 50.2 %copy-start.158 = (f32[16,4,8]{2,0,1:T(8,128)S(1)}, f32[16,4,8]{2,0,1:T(8,128)}, u32[]{:S(2)}) copy-start(f32[16,4,8]{2,0,1:T(8,128)} %copy-done.157) | copy-start | bytes 6148
  565.2 44.6 %copy-start.13 = (bf16[1,256,512]{1,2,0:T(8,128)(2,1)}, bf16[1,256,512]{1,2,0:T(8,128)(2,1)S(1)}, u32[]{:S(2)}) copy-start(bf16[1,256,512]{1,2,0:T(8,128)(2,1)S(1)} %copy.1241) | copy-start | bytes 786436
  565.2 43.3 %copy-start.181 = (f32[16,4,8]{2,0,1:T(8,128)S(1)}, f32[16,4,8]{2,0,1:T(8,128)}, u32[]{:S(2)}) copy-start(f32[16,4,8]{2,0,1:T(8,128)} %get-tuple-element.90) | copy-start | bytes 6148
  565.2 43.9 %copy-start.186 = (f32[16,4,8]{2,0,1:T(8,128)S(1)}, f32[16,4,8]{2,0,1:T(8,128)}, u32[]{:S(2)}) copy-start(f32[16,4,8]{2,0,1:T(8,128)} %get-tuple-element.82) | copy-start | bytes 6148
  565.2 44.5 %copy-start.190 = (f32[16,4,8]{2,0,1:T(8,128)S(1)}, f32[16,4,8]{2,0,1:T(8,128)}, u32[]{:S(2)}) copy-start(f32[16,4,8]{2,0,1:T(8,128)} %get-tuple-element.74) | copy-start | bytes 6148
  565.2 32.0 %all-to-all-start.10 = ((f32[64,1,32]{2,1,0:T(1,128)}), f32[64,1,32]{2,1,0:T(1,128)}, u32[]{:S(2)}, u32[]{:S(2)}) async-start(f32[64,1,32]{2,1,0:T(1,128)} %copy.1009), calls=%async_computation.10 | async-start | bytes 65536 | tf_op jit(solution)/shard_map/all_to_all | solution.py:69
  587.4 47.5 %copy-start.62 = (f32[16,1,4,8,256]{4,3,0,2,1:T(8,128)S(1)}, f32[16,1,4,8,256]{4,3,0,2,1:T(8,128)}, u32[]{:S(2)}) copy-start(f32[16,1,4,8,256]{4,3,0,2,1:T(8,128)} %copy-done.61) | copy-start | bytes 1572868
  587.4 47.5 %copy-start.154 = (f32[16,4,8]{2,0,1:T(8,128)S(1)}, f32[16,4,8]{2,0,1:T(8,128)}, u32[]{:S(2)}) copy-start(f32[16,4,8]{2,0,1:T(8,128)} %copy-done.153) | copy-start | bytes 6148
  597.3 27.8 %all-to-all-start.9 = ((f32[64,1,32]{2,1,0:T(1,128)}), f32[64,1,32]{2,1,0:T(1,128)}, u32[]{:S(2)}, u32[]{:S(2)}) async-start(f32[64,1,32]{2,1,0:T(1,128)} %copy.998), calls=%async_computation.9 | async-start | bytes 65536 | tf_op jit(solution)/shard_map/all_to_all | solution.py:69
  616.1 45.8 %copy-start.146 = (f32[16,4,8]{2,0,1:T(8,128)S(1)}, f32[16,4,8]{2,0,1:T(8,128)}, u32[]{:S(2)}) copy-start(f32[16,4,8]{2,0,1:T(8,128)} %copy-done.145) | copy-start | bytes 6148
  625.0 40.3 %copy-start.16 = (bf16[1,256,512]{1,2,0:T(8,128)(2,1)}, bf16[1,256,512]{1,2,0:T(8,128)(2,1)S(1)}, u32[]{:S(2)}) copy-start(bf16[1,256,512]{1,2,0:T(8,128)(2,1)S(1)} %copy.1242) | copy-start | bytes 786436
  625.1 39.6 %copy-start.175 = (f32[16,4,8]{2,0,1:T(8,128)S(1)}, f32[16,4,8]{2,0,1:T(8,128)}, u32[]{:S(2)}) copy-start(f32[16,4,8]{2,0,1:T(8,128)} %get-tuple-element.80) | copy-start | bytes 6148
  625.1 39.6 %copy-start.178 = (f32[16,4,8]{2,0,1:T(8,128)S(1)}, f32[16,4,8]{2,0,1:T(8,128)}, u32[]{:S(2)}) copy-start(f32[16,4,8]{2,0,1:T(8,128)} %get-tuple-element.72) | copy-start | bytes 6148
  625.1 40.2 %copy-start.183 = (f32[16,4,8]{2,0,1:T(8,128)S(1)}, f32[16,4,8]{2,0,1:T(8,128)}, u32[]{:S(2)}) copy-start(f32[16,4,8]{2,0,1:T(8,128)} %get-tuple-element.64) | copy-start | bytes 6148
  625.1 27.7 %all-to-all-start.8 = ((f32[64,1,32]{2,1,0:T(1,128)}), f32[64,1,32]{2,1,0:T(1,128)}, u32[]{:S(2)}, u32[]{:S(2)}) async-start(f32[64,1,32]{2,1,0:T(1,128)} %copy.987), calls=%async_computation.8 | async-start | bytes 65536 | tf_op jit(solution)/shard_map/all_to_all | solution.py:69
  642.9 47.3 %copy-start.55 = (f32[16,1,4,8,256]{4,3,0,2,1:T(8,128)S(1)}, f32[16,1,4,8,256]{4,3,0,2,1:T(8,128)}, u32[]{:S(2)}) copy-start(f32[16,1,4,8,256]{4,3,0,2,1:T(8,128)} %copy-done.54) | copy-start | bytes 1572868
  642.9 47.3 %copy-start.144 = (f32[16,4,8]{2,0,1:T(8,128)S(1)}, f32[16,4,8]{2,0,1:T(8,128)}, u32[]{:S(2)}) copy-start(f32[16,4,8]{2,0,1:T(8,128)} %copy-done.143) | copy-start | bytes 6148
  652.8 27.9 %all-to-all-start.3 = ((f32[64,1,32]{2,1,0:T(1,128)}), f32[64,1,32]{2,1,0:T(1,128)}, u32[]{:S(2)}, u32[]{:S(2)}) async-start(f32[64,1,32]{2,1,0:T(1,128)} %copy.881), calls=%async_computation.3 | async-start | bytes 65536 | tf_op jit(solution)/shard_map/all_to_all | solution.py:68
  671.1 40.8 %copy-start.138 = (f32[16,4,8]{2,0,1:T(8,128)S(1)}, f32[16,4,8]{2,0,1:T(8,128)}, u32[]{:S(2)}) copy-start(f32[16,4,8]{2,0,1:T(8,128)} %copy-done.137) | copy-start | bytes 6148
  680.6 22.4 %all-to-all-start.2 = ((f32[64,1,32]{2,1,0:T(1,128)}), f32[64,1,32]{2,1,0:T(1,128)}, u32[]{:S(2)}, u32[]{:S(2)}) async-start(f32[64,1,32]{2,1,0:T(1,128)} %copy.854), calls=%async_computation.2 | async-start | bytes 65536 | tf_op jit(solution)/shard_map/all_to_all | solution.py:68
  692.1 42.6 %copy-start.120 = (f32[16,4,8]{2,0,1:T(8,128)S(1)}, f32[16,4,8]{2,0,1:T(8,128)}, u32[]{:S(2)}) copy-start(f32[16,4,8]{2,0,1:T(8,128)} %copy-done.119) | copy-start | bytes 6148
  703.0 22.4 %all-to-all-start.1 = ((f32[64,1,32]{2,1,0:T(1,128)}), f32[64,1,32]{2,1,0:T(1,128)S(1)}, u32[]{:S(2)}, u32[]{:S(2)}) async-start(f32[64,1,32]{2,1,0:T(1,128)} %copy.827), calls=%async_computation.1 | async-start | bytes 65536 | tf_op jit(solution)/shard_map/all_to_all | solution.py:68
  725.5 34.8 %all-to-all-start = ((f32[64,1,32]{2,1,0:T(1,128)}), f32[64,1,32]{2,1,0:T(1,128)S(1)}, u32[]{:S(2)}, u32[]{:S(2)}) async-start(f32[64,1,32]{2,1,0:T(1,128)} %copy.800), calls=%async_computation | async-start | bytes 65536 | tf_op jit(solution)/shard_map/all_to_all | solution.py:68
  760.2 38.7 %all-to-all-start.7 = ((f32[64,1,4096]{2,1,0:T(1,128)}), f32[64,1,4096]{2,1,0:T(1,128)}, u32[]{:S(2)}, u32[]{:S(2)}) async-start(f32[64,1,4096]{2,1,0:T(1,128)} %bitcast.538), calls=%async_computation.7 | async-start | bytes 2097152 | tf_op jit(solution)/shard_map/all_to_all | solution.py:67
  799.0 36.3 %all-to-all-start.6 = ((f32[64,1,4096]{2,1,0:T(1,128)}), f32[64,1,4096]{2,1,0:T(1,128)}, u32[]{:S(2)}, u32[]{:S(2)}) async-start(f32[64,1,4096]{2,1,0:T(1,128)} %bitcast.472), calls=%async_computation.6 | async-start | bytes 2097152 | tf_op jit(solution)/shard_map/all_to_all | solution.py:67
  835.3 108.6 %all-to-all-start.5 = ((f32[64,1,4096]{2,1,0:T(1,128)}), f32[64,1,4096]{2,1,0:T(1,128)}, u32[]{:S(2)}, u32[]{:S(2)}) async-start(f32[64,1,4096]{2,1,0:T(1,128)} %bitcast.406), calls=%async_computation.5 | async-start | bytes 2097152 | tf_op jit(solution)/shard_map/all_to_all | solution.py:67
  943.9 58.1 %all-to-all-start.4 = ((f32[64,1,4096]{2,1,0:T(1,128)}), f32[64,1,4096]{2,1,0:T(1,128)}, u32[]{:S(2)}, u32[]{:S(2)}) async-start(f32[64,1,4096]{2,1,0:T(1,128)} %bitcast.340), calls=%async_computation.4 | async-start | bytes 2097152 | tf_op jit(solution)/shard_map/all_to_all | solution.py:67
  952.9 158.9 %all-gather.2.cloned.1.call-start = ((), (), s32[]{:S(2)}) async-start(), calls=%async_computation.12 | async-start | bytes 2129920 | tf_op jit(solution)/shard_map/all_gather | solution.py:177
  955.8 45.2 %copy-start.206 = (f32[64,1,32]{2,1,0:T(1,128)S(1)}, f32[64,1,32]{2,1,0:T(1,128)}, u32[]{:S(2)}) copy-start(f32[64,1,32]{2,1,0:T(1,128)} %copy-done.205) | copy-start | bytes 24580
  955.8 46.0 %copy-start.243 = (bf16[1,4,512]{2,1,0:T(4,128)(2,1)S(1)}, bf16[1,4,512]{2,1,0:T(4,128)(2,1)}, u32[]{:S(2)}) copy-start(bf16[1,4,512]{2,1,0:T(4,128)(2,1)} %param.12) | copy-start | bytes 12292
  (225 other events, 1731.9 us)
Sparse Core Ops, SparseCore 0:
  1006.8 104.9 all-gather.1
where the time goes:
time: 1150 us; the launch traced here: 1130 us
  blocking collectives  369 us (32%)
  local copies, waits for them, and re-layouts  245 us (21%)
  other arithmetic  204 us (18%)
  starting transfers between devices  109 us (9%)
  waiting for transfers between devices  105 us (9%)
  matrix products  83.1 us (7%)
  between operations  19.2 us (2%)
    all_gather x4, blocking collectives, local(): lax.all_gather(queries[:, step_index:step_index + 1], 'req', axis=0, tile...  341 us
    all_gather x1, waiting for transfers between devices, local(): piece_rows = lax.all_gather(attention, 'req', axis=0, tiled=True)  105 us
    scatter-add x32, other arithmetic, prefix_partials(): out_all.at[slot_rows].add(jnp.where(is_valid[..., None], part_out, 0.0))  77.8 us
    gather x4, local copies, waits for them, and re-layouts, local(): key_table[pick_list.T, head_index_list]  66.9 us
    dot_general x32, matrix products, prefix_partials(): jnp.einsum('cskgl,lkd->cskgd', weights, stretch_values, preferred_element...  44.8 us
    gather x1, local copies, waits for them, and re-layouts, local(): value_table[pick_list.T, head_index_list]  40.2 us
    scatter-add x32, other arithmetic, prefix_partials(): total_all = total_all.at[slot_rows].add(jnp.where(is_valid, row_total, 0.0))  39.8 us
    scatter-add x32, other arithmetic, prefix_partials(): peak_all = peak_all.at[slot_rows].add(jnp.where(is_valid, row_peak, 0.0))  39.8 us
  transfers between devices with their start and end apart: 13, of which 1 were waited for; matrix products, arithmetic and copies ran while one was open for 33% of the time, Pallas kernels for 0%

commit v1 on v0

v1 whole, which is shorter than its diff:
```python
import functools

import jax
import jax.numpy as jnp
from jax import lax
from jax.experimental import pallas as pl
from jax.experimental.pallas import tpu as pltpu
from jax.sharding import PartitionSpec as P

HEAD = 128
PROMPTS = 8
STEPS = 4
ROWS = 32
REQS = 64
CHIPS = 32
PORTION = 256
HISTORY = 2048
KEPT = 1024
PAY = 136
LOG2E = 1.4426950408889634
C2 = HEAD ** -0.5 * LOG2E
NEG = -1e30
BF = jnp.bfloat16
F32 = jnp.float32

SAME_CORE = [[2 * i + c for i in range(CHIPS)] for c in range(2)]
CORE_SWAP = [(i, i ^ 1) for i in range(REQS)]

VM = pl.BlockSpec(memory_space=pltpu.VMEM)
SM = pl.BlockSpec(memory_space=pltpu.SMEM)
HB = pl.BlockSpec(memory_space=pl.ANY)


def nt(a, b):
    return lax.dot_general(a, b, (((1,), (1,)), ((), ())), preferred_element_type=F32)


def mm(a, b):
    return lax.dot_general(a, b, (((1,), (0,)), ((), ())), preferred_element_type=F32)


def iota(shape, dim):
    return lax.broadcasted_iota(jnp.int32, shape, dim)


def pack_kernel(mem_ref, q_ref, out_ref, tmp):
    for head in range(32):
        tmp[pl.ds(head * STEPS, STEPS), :] = q_ref[0, :, pl.ds(head * HEAD, HEAD)].astype(F32)
    data = tmp[...].astype(BF)
    side = jnp.full((8, HEAD), mem_ref[0, 0], jnp.int32).astype(F32).astype(BF)
    for i in range(CHIPS):
        out_ref[i, pl.ds(0, 128), :] = data
        out_ref[i, pl.ds(128, 8), :] = side


def pack(membership, queries):
    return pl.pallas_call(
        pack_kernel,
        out_shape=jax.ShapeDtypeStruct((CHIPS, PAY, HEAD), BF),
        in_specs=[SM, VM],
        out_specs=VM,
        scratch_shapes=[pltpu.VMEM((128, HEAD), F32)],
        name="pack",
    )(membership, queries)


def private_kernel(q_ref, kept_ref, hk_ref, hv_ref, nk_ref, nv_ref, o_ref, l_ref, knew, vnew):
    ones = jnp.ones((HISTORY, HEAD), BF)
    ones_new = jnp.ones((128, HEAD), BF)
    sub_hi = iota((16, KEPT), 0)
    sub_lo = iota((128, KEPT), 0)
    col = iota((ROWS, 128), 1)
    step_of = iota((ROWS, 128), 0) & (STEPS - 1)
    new_ok = (col < STEPS) & (col <= step_of)
    knew[...] = jnp.zeros_like(knew)
    vnew[...] = jnp.zeros_like(vnew)
    for g in range(4):
        lanes = pl.ds(g * HEAD, HEAD)
        pos = kept_ref[0, pl.ds(g, 1), :]
        hot_hi = jnp.where(sub_hi == lax.shift_right_logical(pos, 7), 1.0, 0.0).astype(BF)
        hot_lo = jnp.where(sub_lo == (pos & 127), 1.0, 0.0).astype(BF)
        count = nt(hot_hi, hot_lo)
        q = q_ref[0, pl.ds(g * ROWS, ROWS), :]
        s = nt(q, hk_ref[0, :, lanes])
        s = jnp.concatenate(
            [
                jnp.where(count[i : i + 1, :] > 0.5, s[:, i * 128 : (i + 1) * 128], NEG)
                for i in range(16)
            ],
            axis=1,
        )
        knew[pl.ds(0, STEPS), :] = nk_ref[0, :, lanes].astype(F32)
        vnew[pl.ds(0, STEPS), :] = nv_ref[0, :, lanes].astype(F32)
        sn = jnp.where(new_ok, nt(q, knew[...].astype(BF)), NEG)
        peak = jnp.maximum(jnp.max(s, axis=1, keepdims=True), jnp.max(sn, axis=1, keepdims=True))
        p = jnp.exp2((s - peak) * C2).astype(BF)
        pn = jnp.exp2((sn - peak) * C2).astype(BF)
        ov = mm(p, jnp.concatenate([hv_ref[0, :, lanes], ones], axis=1))
        ov += mm(pn, jnp.concatenate([vnew[...].astype(BF), ones_new], axis=1))
        total = ov[:, HEAD:]
        o_ref[g] = ov[:, :HEAD] / total
        l_ref[g] = peak * C2 + jnp.log(total) * LOG2E


def private(packed, kept, hk, hv, nk, nv):
    return pl.pallas_call(
        private_kernel,
        out_shape=[jax.ShapeDtypeStruct((4, ROWS, HEAD), F32)] * 2,
        in_specs=[VM] * 6,
        out_specs=[VM] * 2,
        scratch_shapes=[pltpu.VMEM((128, HEAD), F32)] * 2,
        cost_estimate=pl.CostEstimate(
            flops=400_000_000, transcendentals=300_000, bytes_accessed=5_000_000
        ),
        name="private",
    )(packed[:1], kept, hk, hv, nk, nv)


def prefix_kernel(
    keep, qa_hbm, qb_hbm, k_hbm, v_hbm, po_ref, pl_ref, o_ref, l_ref,
    q, kbuf, vbuf, obuf, lbuf, tab_v, tab_s, qsem, ksem, tsem,
):
    me = lax.axis_index("req")
    core = me & 1
    pair = core if keep else 1 - core
    ca = pltpu.make_async_copy(qa_hbm, q.at[pl.ds(0, CHIPS)], qsem.at[0])
    cb = pltpu.make_async_copy(qb_hbm, q.at[pl.ds(CHIPS, CHIPS)], qsem.at[1])
    ca.start()
    cb.start()
    lanes = pl.ds(pl.multiple_of(pair * 256, 256), 256)

    def fetch(p):
        return (
            pltpu.make_async_copy(k_hbm.at[p, :, lanes], kbuf.at[p], ksem.at[p, 0]),
            pltpu.make_async_copy(v_hbm.at[p, :, lanes], vbuf.at[p], ksem.at[p, 1]),
        )

    for p in range(PROMPTS):
        for copy in fetch(p):
            copy.start()
    ca.wait()
    cb.wait()

    sides = q[:, pl.ds(128, 8), :].astype(F32)
    member = jnp.max(sides, axis=1)
    member = jnp.concatenate([member, jnp.full((64, HEAD), 99.0, F32)], axis=0)
    across = member.T
    row, lane = iota((128, 128), 0), iota((128, 128), 1)
    before = (across < member) | ((across == member) & (lane < row))
    slot = jnp.sum(jnp.where(before, 1.0, 0.0), axis=1, keepdims=True)
    here = slot == lane.astype(F32)
    rowf = row.astype(F32)
    coref = core.astype(F32)
    req = jnp.where(row < CHIPS, 2.0 * rowf + coref, 2.0 * (rowf - CHIPS) + 1.0 - coref)
    lanef = lane.astype(F32)

    def total(x):
        return jnp.sum(x, axis=0, keepdims=True)

    order = total(jnp.where(here & (row < REQS), rowf, 0.0))
    target = total(jnp.where(here, jnp.where(row < REQS, req, float(REQS)), 0.0))
    starts = total(jnp.where(member < lanef, 1.0, 0.0))
    counts = total(jnp.where(member == lanef, 1.0, 0.0))
    table = jnp.concatenate([order, target, starts, counts, jnp.zeros((4, 128), F32)], axis=0)
    tab_v[...] = table.astype(jnp.int32)
    ct = pltpu.make_async_copy(tab_v, tab_s, tsem)
    ct.start()
    ct.wait()

    ones = jnp.ones((PORTION, HEAD), BF)
    qrow = pl.multiple_of(pair * 64, 64)

    for p in range(PROMPTS):
        for copy in fetch(p):
            copy.wait()
        start = tab_s[2, p]
        chunks = lax.shift_right_logical(tab_s[3, p] + 7, 3)

        def chunk(i, carry):
            slot0 = start + i * 8
            for head in range(2):
                rows = pl.ds(qrow + head * ROWS, ROWS)
                qs = jnp.concatenate([q[tab_s[0, slot0 + j], rows, :] for j in range(8)], axis=0)
                s = nt(qs, kbuf[p, :, pl.ds(head * HEAD, HEAD)])
                peak = jnp.max(s, axis=1, keepdims=True)
                w = jnp.exp2((s - peak) * C2).astype(BF)
                ov = mm(w, jnp.concatenate([vbuf[p, :, pl.ds(head * HEAD, HEAD)], ones], axis=1))
                l = ov[:, HEAD:]
                o = ov[:, :HEAD] / l
                lse = peak * C2 + jnp.log(l) * LOG2E
                for j in range(8):
                    t = tab_s[1, slot0 + j]
                    obuf[head, t] = o[j * ROWS : (j + 1) * ROWS]
                    lbuf[head, t] = lse[j * ROWS : (j + 1) * ROWS]
            return carry

        lax.fori_loop(0, chunks, chunk, 0)

    for head in range(2):
        o1, l1 = obuf[head, me], lbuf[head, me]
        o2, l2 = po_ref[pair * 2 + head], pl_ref[pair * 2 + head]
        top = jnp.maximum(l1, l2)
        e1, e2 = jnp.exp2(l1 - top), jnp.exp2(l2 - top)
        both = e1 + e2
        obuf[head, me] = (e1 * o1 + e2 * o2) / both
        lbuf[head, me] = top + jnp.log(both) * LOG2E

    diag = row == lane
    for head in range(2):
        for grp in range(16):
            n = head * 16 + grp
            lb = lbuf[head, pl.ds(grp * 4, 4)].reshape(128, HEAD)
            l_ref[pl.ds(n, 1), :] = total(jnp.where(diag, lb, 0.0))
            ob = obuf[head, pl.ds(grp * 4, 4)].reshape(128, HEAD)
            o_ref[n] = ob.astype(o_ref.dtype)


def prefix(keep, qa, qb, k, v, po, pll):
    return pl.pallas_call(
        functools.partial(prefix_kernel, keep),
        out_shape=[
            jax.ShapeDtypeStruct((32, 128, HEAD), F32 if keep else BF),
            jax.ShapeDtypeStruct((32, 128), F32),
        ],
        in_specs=[HB, HB, HB, HB, VM, VM],
        out_specs=[VM, VM],
        scratch_shapes=[
            pltpu.VMEM((REQS, PAY, HEAD), BF),
            pltpu.VMEM((PROMPTS, PORTION, 256), BF),
            pltpu.VMEM((PROMPTS, PORTION, 256), BF),
            pltpu.VMEM((2, REQS + 1, ROWS, HEAD), F32),
            pltpu.VMEM((2, REQS + 1, ROWS, HEAD), F32),
            pltpu.VMEM((8, 128), jnp.int32),
            pltpu.SMEM((8, 128), jnp.int32),
            pltpu.SemaphoreType.DMA((2,)),
            pltpu.SemaphoreType.DMA((PROMPTS, 2)),
            pltpu.SemaphoreType.DMA(()),
        ],
        cost_estimate=pl.CostEstimate(
            flops=600_000_000, transcendentals=1_000_000, bytes_accessed=6_000_000
        ),
        name="prefix_keep" if keep else "prefix_send",
    )(qa, qb, k, v, po, pll)


def merge_kernel(o1_ref, l1_ref, o2_ref, l2_ref, out_ref):
    l1, l2 = l1_ref[...], l2_ref[...]
    top = jnp.maximum(l1, l2)
    e1, e2 = jnp.exp2(l1 - top), jnp.exp2(l2 - top)
    both = e1 + e2
    w1 = e1 / both
    lse = top + jnp.log(both) * LOG2E
    hi = lse.astype(BF).astype(F32)
    mid = (lse - hi).astype(BF).astype(F32)
    lo = lse - hi - mid
    cols = jnp.concatenate([w1, jnp.zeros((96, 128), F32)], axis=0).T
    sub = iota((8, 128), 0)
    for n in range(32):
        w = cols[:, n : n + 1]
        o2 = o2_ref[n].astype(F32)
        out_ref[n, pl.ds(0, 128), :] = (o2 + w * (o1_ref[n] - o2)).astype(BF)
        side = jnp.where(
            sub == 0, hi[n : n + 1], jnp.where(sub == 1, mid[n : n + 1], jnp.where(sub == 2, lo[n : n + 1], 0.0))
        )
        out_ref[n, pl.ds(128, 8), :] = side.astype(BF)


def merge(o1, l1, o2, l2):
    return pl.pallas_call(
        merge_kernel,
        out_shape=jax.ShapeDtypeStruct((CHIPS, PAY, HEAD), BF),
        in_specs=[VM] * 4,
        out_specs=VM,
        name="merge",
    )(o1, l1, o2, l2)


def combine_kernel(in_ref, out_ref, acc_ref):
    pieces = [in_ref[n, pl.ds(128, 8), :].astype(F32) for n in range(CHIPS)]
    lse = jnp.concatenate([x[0:1] + x[1:2] + x[2:3] for x in pieces], axis=0)
    top = jnp.max(lse, axis=0, keepdims=True)
    e = jnp.exp2(lse - top)
    w = e / jnp.sum(e, axis=0, keepdims=True)
    cols = jnp.concatenate([w, jnp.zeros((96, 128), F32)], axis=0).T
    acc = jnp.zeros((128, HEAD), F32)
    for n in range(CHIPS):
        acc += cols[:, n : n + 1] * in_ref[n, pl.ds(0, 128), :].astype(F32)
    for r in range(4):
        for h in range(8):
            at = r * ROWS + h * STEPS
            acc_ref[pl.ds(h * 16 + r * STEPS, STEPS), :] = acc[at : at + STEPS]
    att = acc_ref[...].astype(BF)
    for n in range(CHIPS):
        out_ref[n] = att


def combine(x):
    return pl.pallas_call(
        combine_kernel,
        out_shape=jax.ShapeDtypeStruct((CHIPS, 128, HEAD), BF),
        in_specs=[VM],
        out_specs=VM,
        scratch_shapes=[pltpu.VMEM((128, HEAD), F32)],
        name="combine",
    )(x)


def project_kernel(own, *refs):
    if own:
        a_ref, w_hbm, out_ref, w, sem = refs
        acc = jnp.zeros((REQS * STEPS, 128), F32)
    else:
        a_ref, w_hbm, base_ref, out_ref, w, sem = refs
        acc = base_ref[...]
    core = lax.axis_index("req") & 1
    pair = core if own else 1 - core
    copy = pltpu.make_async_copy(w_hbm.at[pl.ds(pl.multiple_of(pair * 2048, 2048), 2048), :], w, sem)
    copy.start()
    copy.wait()
    for z in range(2):
        for h in range(0, 8, 2):
            a = jnp.concatenate(
                [
                    a_ref[pl.ds(z * 16, 16), pl.ds((h + i) * 16, 16), :].reshape(256, HEAD)
                    for i in range(2)
                ],
                axis=1,
            )
            acc += mm(a, w[pl.ds((z * 8 + h) * 128, 256), :])
    out_ref[...] = acc


def project(own, a, w, *base):
    return pl.pallas_call(
        functools.partial(project_kernel, own),
        out_shape=jax.ShapeDtypeStruct((REQS * STEPS, 128), F32),
        in_specs=[VM, HB] + [VM] * len(base),
        out_specs=VM,
        scratch_shapes=[pltpu.VMEM((2048, 128), BF), pltpu.SemaphoreType.DMA(())],
        cost_estimate=pl.CostEstimate(
            flops=140_000_000, transcendentals=0, bytes_accessed=2_000_000
        ),
        name="project_own" if own else "project_other",
    )(a, w, *base)


def over_chips(x):
    return lax.all_to_all(
        x, "req", split_axis=0, concat_axis=0, axis_index_groups=SAME_CORE, tiled=True
    )


def swap_cores(x):
    return lax.ppermute(x, "req", CORE_SWAP)


def local(queries, nk, nv, pk, pv, hk, hv, kept, membership, out_weight):
    packed = pack(membership, queries)
    qa = over_chips(packed)
    qb = swap_cores(qa)
    po, pll = private(packed, kept, hk, hv, nk, nv)
    send_o, send_l = prefix(False, qa, qb, pk, pv, po, pll)
    got_o, got_l = swap_cores(send_o), swap_cores(send_l)
    keep_o, keep_l = prefix(True, qa, qb, pk, pv, po, pll)
    parts = over_chips(merge(keep_o, keep_l, got_o, got_l))
    att = over_chips(combine(parts))
    att_other = swap_cores(att)
    half = project(True, att, out_weight)
    mine = project(False, att_other, out_weight, half)
    theirs = lax.ppermute(mine, "kvh", [(0, 1), (1, 0)])
    return (mine + theirs).astype(BF).reshape(REQS, STEPS, 128)


def solution(mesh):
    placed = (
        P("req", None, "kvh"),
        P("req", None, "kvh"),
        P("req", None, "kvh"),
        P(None, "req", "kvh"),
        P(None, "req", "kvh"),
        P("req", None, "kvh"),
        P("req", None, "kvh"),
        P("req", "kvh", None),
        P("req", None),
        P("kvh", "req"),
    )
    return jax.shard_map(
        local, mesh=mesh, in_specs=placed, out_specs=P(None, None, "req"), check_vma=False
    )
```

time: 1150 us -> 132 us (0.11); the launches traced: 1130 us -> 130 us
  blocking collectives: 369 us -> 68.9 us
  local copies, waits for them, and re-layouts: 245 us -> 4.35 us
  other arithmetic: 204 us -> 1.56 us
  waiting for transfers between devices: 105 us -> 3.13 us
  starting transfers between devices: 109 us -> 8.54 us
  matrix products: 83.1 us -> 0 us
  Pallas kernels: 0 us -> 43.2 us
  between operations: 19.2 us -> 0.75 us
    all_gather x4 -> x0, blocking collectives: 341 us -> none  [local(): lax.all_gather(queries[:, step_index:step_index + 1], 'req', axis=0, tile...]
    scatter-add x96 -> x0, other arithmetic: 158 us -> none  [the longest x32 77.8 us: prefix_partials(): out_all.at[slot_rows].add(jnp.where(is_valid[..., None], part_out, 0.0))]
    gather x45 -> x0, local copies, waits for them, and re-layouts: 150 us -> none  [the longest x4 66.9 us: local(): key_table[pick_list.T, head_index_list]]
    all_to_all x12 -> x0, starting transfers between devices: 109 us -> none  [the longest x4 38 us: return_partials(): lax.all_to_all(flat_out, 'req', split_axis=0, concat_axis=0, tiled=True)]
    all_gather x1 -> x0, waiting for transfers between devices: 105 us -> none  [local(): piece_rows = lax.all_gather(attention, 'req', axis=0, tiled=True)]
    dot_general x69 -> x0, matrix products: 83.1 us -> none  [the longest x32 44.8 us: prefix_partials(): jnp.einsum('cskgl,lkd->cskgd', weights, stretch_values, preferred_element...]
    all_to_all x0 -> x3, blocking collectives: none -> 68.9 us  [over_chips(): lax.all_to_all(x, 'req', split_axis=0, concat_axis=0, axis_index_groups=S...]
    pallas_call x0 -> x8, Pallas kernels: none -> 43.2 us  [the longest x2 22.1 us: prefix(): pl.pallas_call(functools.partial(prefix_kernel, keep), out_shape=[jax.Sha...]
  transfers between devices with their start and end apart: 13 -> 5, of which waited for: 1 -> 1; matrix products, arithmetic and copies ran while one was open for 33% -> 1% of each run, Pallas kernels for 0% -> 16%
where the time goes in v1:
time: 132 us; the launch traced here: 130 us
  blocking collectives  68.9 us (52%)
  Pallas kernels  43.2 us (33%)
  starting transfers between devices  8.54 us (6%)
  local copies, waits for them, and re-layouts  4.35 us (3%)
  waiting for transfers between devices  3.13 us (2%)
  other arithmetic  1.56 us (1%)
    all_to_all x3, blocking collectives, over_chips(): lax.all_to_all(x, 'req', split_axis=0, concat_axis=0, axis_index_groups=S...  68.9 us
    pallas_call x2, Pallas kernels, prefix(): pl.pallas_call(functools.partial(prefix_kernel, keep), out_shape=[jax.Sha...  22.1 us
    pallas_call x2, Pallas kernels, project(): pl.pallas_call(functools.partial(project_kernel, own), out_shape=jax.Shap...  6.69 us
    pallas_call x1, Pallas kernels, private(): pl.pallas_call(private_kernel, out_shape=[jax.ShapeDtypeStruct((4, ROWS,...  5.66 us
    ppermute x4, starting transfers between devices, swap_cores(): return lax.ppermute(x, 'req', CORE_SWAP)  5.16 us
    pallas_call x1, Pallas kernels, merge(): pl.pallas_call(merge_kernel, out_shape=jax.ShapeDtypeStruct((CHIPS, PAY,...  3.65 us
    ppermute x1, starting transfers between devices, local(): theirs = lax.ppermute(mine, 'kvh', [(0, 1), (1, 0)])  3.38 us
    pallas_call x1, Pallas kernels, combine(): pl.pallas_call(combine_kernel, out_shape=jax.ShapeDtypeStruct((CHIPS, 128...  3.22 us
  transfers between devices with their start and end apart: 5, of which 1 were waited for; matrix products, arithmetic and copies ran while one was open for 1% of the time, Pallas kernels for 16%

profile of v1, /device:TPU:1, one launch (start us, length us, event | category | flops | bytes accessed | tf_op | source)
XLA Modules:
  0.0 130.5 jit_solution(9517423388942081457)
XLA Ops:
  0.7 1.8 %pack.1 = bf16[32,136,128]{2,1,0:T(8,128)(2,1)} custom-call(s32[1,1]{1,0:T(1,128)S(6)} %copy.11.mem_ref, bf16[1,4,4096]{2,1,0:T(4,128)(2,1)} %q_ref.1), custom_call_target="tpu_custom_call" | custom-call | tf_op jit(solution)/shard_map/pack/pallas_call | solution.py:57
  2.5 27.0 %all_to_all.15.qa_hbm = bf16[32,136,128]{2,1,0:T(8,128)(2,1)S(1)} all-to-all(bf16[32,136,128]{2,1,0:T(8,128)(2,1)} %pack.1), channel_id=1, replica_groups={{0,4,8,12,16,20,24,28,32,36,40,44,48,52,56,60,64,68,72,76,80,84,88,92,9..., dimensions={0} | all-to-all | bytes 2228224 | tf_op jit(solution)/shard_map/all_to_all | solution.py:348
  29.5 1.7 %collective-permute-start = (bf16[32,136,128]{2,1,0:T(8,128)(2,1)S(1)}, bf16[32,136,128]{2,1,0:T(8,128)(2,1)S(1)}, u32[]{:S(2)}, u32[]{:S(2)}) collective-permute-start(bf16[32,136,128]{2,1,0:T(8,128)(2,1)S(1)} %all_to_all.15.qa_hbm), channel_id=1, source_target_pairs={{0,2},{2,0},{4,6},{6,4},{8,10},{10,8},{12,14},{14,12},{16,18},{18,... | collective-permute-start | bytes 3342344 | tf_op jit(solution)/shard_map/ppermute | solution.py:354
  31.2 1.4 %slice.4.q_ref = bf16[1,136,128]{2,1,0:T(8,128)(2,1)} slice(bf16[32,136,128]{2,1,0:T(8,128)(2,1)} %pack.1), slice={[0:1], [0:136], [0:128]} | slice | bytes 69632 | tf_op jit(solution)/shard_map/slice | solution.py:116
  32.6 5.7 %private.1 = (f32[4,32,128]{2,1,0:T(8,128)}, f32[4,32,128]{2,1,0:T(8,128)}) custom-call(bf16[1,136,128]{2,1,0:T(8,128)(2,1)} %slice.4.q_ref, s32[1,4,1024]{2,1,0:T(4,128)} %kept_ref.1, bf16[1,2048,512]{2,1,0:T(8,128)(2,1)} %hk_ref.1, bf16[1,2048,512]{2,1,0:T(8,128)(2,1)} %hv_ref.1, bf16[1,4,512]{2,1,0:T(4,128)(2,1)} %nk_ref.1, bf16[1,4,512]{2,1,0:T(4,128)(2,1)} %nv_ref.1), custom_call_target="tpu_custom_call" | custom-call | flops 400000000 | bytes 5000000 | tf_op jit(solution)/shard_map/private/pallas_call | solution.py:106
  38.2 0.0 copy-done
  38.2 0.0 collective-permute-done.qb_hbm
  38.2 0.0 copy-start.1
  38.2 1.0 copy-done.1
  39.2 10.9 %prefix_send.1 = (bf16[32,128,128]{2,1,0:T(8,128)(2,1)}, f32[32,128]{1,0:T(8,128)}) custom-call(bf16[32,136,128]{2,1,0:T(8,128)(2,1)} %copy-done, bf16[32,136,128]{2,1,0:T(8,128)(2,1)} %copy-done.1, bf16[8,256,512]{2,1,0:T(8,128)(2,1)} %k_hbm.3, bf16[8,256,512]{2,1,0:T(8,128)(2,1)} %v_hbm.3, f32[4,32,128]{2,1,0:T(8,128)} %get-tuple-element.11.po_ref, ...), custom_call_target="tpu_custom_call" | custom-call | flops 600000000 | bytes 6000000 | tf_op jit(solution)/shard_map/prefix_send/pallas_call | solution.py:219
  50.1 0.1 collective-permute-start.1
  50.2 0.5 collective-permute-start.2
  50.7 11.2 %prefix_keep.1 = (f32[32,128,128]{2,1,0:T(8,128)}, f32[32,128]{1,0:T(8,128)}) custom-call(bf16[32,136,128]{2,1,0:T(8,128)(2,1)} %copy-done, bf16[32,136,128]{2,1,0:T(8,128)(2,1)} %copy-done.1, bf16[8,256,512]{2,1,0:T(8,128)(2,1)} %k_hbm.3, bf16[8,256,512]{2,1,0:T(8,128)(2,1)} %v_hbm.3, f32[4,32,128]{2,1,0:T(8,128)} %get-tuple-element.11.po_ref, ...), custom_call_target="tpu_custom_call" | custom-call | flops 600000000 | bytes 6000000 | tf_op jit(solution)/shard_map/prefix_keep/pallas_call | solution.py:219
  62.0 0.0 collective-permute-done.2.l2_ref
  62.0 0.0 copy-start.5
  62.0 0.0 collective-permute-done.1.o2_ref
  62.0 0.0 copy-start.4
  62.0 0.6 copy-done.5
  62.6 0.4 copy-done.4
  63.0 3.7 %merge.1 = bf16[32,136,128]{2,1,0:T(8,128)(2,1)} custom-call(f32[32,128,128]{2,1,0:T(8,128)} %get-tuple-element.13.o1_ref, f32[32,128]{1,0:T(8,128)} %get-tuple-element.14.l1_ref, bf16[32,128,128]{2,1,0:T(8,128)(2,1)} %copy-done.4, f32[32,128]{1,0:T(8,128)} %copy-done.5), custom_call_target="tpu_custom_call" | custom-call | tf_op jit(solution)/shard_map/merge/pallas_call | solution.py:269
  66.7 23.2 %all_to_all.16.in_ref = bf16[32,136,128]{2,1,0:T(8,128)(2,1)} all-to-all(bf16[32,136,128]{2,1,0:T(8,128)(2,1)} %merge.1), channel_id=1, replica_groups={{0,4,8,12,16,20,24,28,32,36,40,44,48,52,56,60,64,68,72,76,80,84,88,92,9..., dimensions={0} | all-to-all | bytes 2228224 | tf_op jit(solution)/shard_map/all_to_all | solution.py:348
  89.9 3.2 %combine.1 = bf16[32,128,128]{2,1,0:T(8,128)(2,1)} custom-call(bf16[32,136,128]{2,1,0:T(8,128)(2,1)} %all_to_all.16.in_ref), custom_call_target="tpu_custom_call" | custom-call | tf_op jit(solution)/shard_map/combine/pallas_call | solution.py:298
  93.1 18.8 %all_to_all.17.refs_0_ = bf16[32,128,128]{2,1,0:T(8,128)(2,1)S(1)} all-to-all(bf16[32,128,128]{2,1,0:T(8,128)(2,1)} %combine.1), channel_id=1, replica_groups={{0,4,8,12,16,20,24,28,32,36,40,44,48,52,56,60,64,68,72,76,80,84,88,92,9..., dimensions={0} | all-to-all | bytes 2097152 | tf_op jit(solution)/shard_map/all_to_all | solution.py:348
  111.9 2.8 %collective-permute-start.3 = (bf16[32,128,128]{2,1,0:T(8,128)(2,1)S(1)}, bf16[32,128,128]{2,1,0:T(8,128)(2,1)S(1)}, u32[]{:S(2)}, u32[]{:S(2)}) collective-permute-start(bf16[32,128,128]{2,1,0:T(8,128)(2,1)S(1)} %all_to_all.17.refs_0_), channel_id=1, source_target_pairs={{0,2},{2,0},{4,6},{6,4},{8,10},{10,8},{12,14},{14,12},{16,18},{18,... | collective-permute-start | bytes 3145736 | tf_op jit(solution)/shard_map/ppermute | solution.py:354
  114.7 0.0 copy-done.2
  114.7 3.3 %project_own.1.refs_2_ = f32[256,128]{1,0:T(8,128)} custom-call(bf16[32,128,128]{2,1,0:T(8,128)(2,1)} %copy-done.2, bf16[4096,128]{1,0:T(8,128)(2,1)} %refs_1_.3), custom_call_target="tpu_custom_call" | custom-call | flops 140000000 | bytes 2000000 | tf_op jit(solution)/shard_map/project_own/pallas_call | solution.py:334
  118.1 0.0 collective-permute-done.3.refs_0_
  118.1 1.0 copy-done.3
  119.0 3.4 %project_other.1 = f32[256,128]{1,0:T(8,128)} custom-call(bf16[32,128,128]{2,1,0:T(8,128)(2,1)} %copy-done.3, bf16[4096,128]{1,0:T(8,128)(2,1)} %refs_1_.3, f32[256,128]{1,0:T(8,128)} %project_own.1.refs_2_), custom_call_target="tpu_custom_call" | custom-call | flops 140000000 | bytes 2000000 | tf_op jit(solution)/shard_map/project_other/pallas_call | solution.py:334
  122.4 3.4 %collective-permute-start.4 = (f32[256,128]{1,0:T(8,128)}, f32[256,128]{1,0:T(8,128)S(1)}, u32[]{:S(2)}, u32[]{:S(2)}) collective-permute-start(f32[256,128]{1,0:T(8,128)} %project_other.1), channel_id=1, source_target_pairs={{0,1},{1,0},{2,3},{3,2},{4,5},{5,4},{6,7},{7,6},{8,9},{9,8},{10,11... | collective-permute-start | bytes 393224 | tf_op jit(solution)/shard_map/ppermute | solution.py:370
  125.8 3.1 %collective-permute-done.4 = f32[256,128]{1,0:T(8,128)S(1)} collective-permute-done((f32[256,128]{1,0:T(8,128)}, f32[256,128]{1,0:T(8,128)S(1)}, u32[]{:S(2)}, u32[]{:S(2)}) %collective-permute-start.4) | collective-permute-done | bytes 131104 | tf_op jit(solution)/shard_map/ppermute | solution.py:370
  128.9 1.6 %add_convert_fusion = bf16[256,128]{1,0:T(8,128)(2,1)} fusion(f32[256,128]{1,0:T(8,128)} %project_other.1, f32[256,128]{1,0:T(8,128)S(1)} %collective-permute-done.4), kind=kLoop, calls=%fused_computation | loop fusion | flops 65536 | bytes 327680 | tf_op jit(solution)/shard_map/convert_element_type | solution.py:371
  (3 shorter events, 0.0 us)
Async XLA Ops:
  29.5 8.8 %copy-start = (bf16[32,136,128]{2,1,0:T(8,128)(2,1)}, bf16[32,136,128]{2,1,0:T(8,128)(2,1)S(1)}, u32[]{:S(2)}) copy-start(bf16[32,136,128]{2,1,0:T(8,128)(2,1)S(1)} %all_to_all.15.qa_hbm) | copy-start | bytes 3342340
  29.5 8.8 %collective-permute-start = (bf16[32,136,128]{2,1,0:T(8,128)(2,1)S(1)}, bf16[32,136,128]{2,1,0:T(8,128)(2,1)S(1)}, u32[]{:S(2)}, u32[]{:S(2)}) collective-permute-start(bf16[32,136,128]{2,1,0:T(8,128)(2,1)S(1)} %all_to_all.15.qa_hbm), channel_id=1, source_target_pairs={{0,2},{2,0},{4,6},{6,4},{8,10},{10,8},{12,14},{14,12},{16,18},{18,... | collective-permute-start | bytes 3342344 | tf_op jit(solution)/shard_map/ppermute | solution.py:354
  38.2 1.0 copy-start.1
  50.1 11.9 %collective-permute-start.1 = (bf16[32,128,128]{2,1,0:T(8,128)(2,1)}, bf16[32,128,128]{2,1,0:T(8,128)(2,1)S(1)}, u32[]{:S(2)}, u32[]{:S(2)}) collective-permute-start(bf16[32,128,128]{2,1,0:T(8,128)(2,1)} %get-tuple-element.15), channel_id=1, source_target_pairs={{0,2},{2,0},{4,6},{6,4},{8,10},{10,8},{12,14},{14,12},{16,18},{18,... | collective-permute-start | bytes 3145736 | tf_op jit(solution)/shard_map/ppermute | solution.py:354
  50.2 11.7 %collective-permute-start.2 = (f32[32,128]{1,0:T(8,128)}, f32[32,128]{1,0:T(8,128)S(1)}, u32[]{:S(2)}, u32[]{:S(2)}) collective-permute-start(f32[32,128]{1,0:T(8,128)} %get-tuple-element.16), channel_id=1, source_target_pairs={{0,2},{2,0},{4,6},{6,4},{8,10},{10,8},{12,14},{14,12},{16,18},{18,... | collective-permute-start | bytes 49160 | tf_op jit(solution)/shard_map/ppermute | solution.py:354
  62.0 0.6 copy-start.5
  62.0 1.0 copy-start.4
  111.9 2.8 %copy-start.2 = (bf16[32,128,128]{2,1,0:T(8,128)(2,1)}, bf16[32,128,128]{2,1,0:T(8,128)(2,1)S(1)}, u32[]{:S(2)}) copy-start(bf16[32,128,128]{2,1,0:T(8,128)(2,1)S(1)} %all_to_all.17.refs_0_) | copy-start | bytes 3145732
  111.9 6.2 %collective-permute-start.3 = (bf16[32,128,128]{2,1,0:T(8,128)(2,1)S(1)}, bf16[32,128,128]{2,1,0:T(8,128)(2,1)S(1)}, u32[]{:S(2)}, u32[]{:S(2)}) collective-permute-start(bf16[32,128,128]{2,1,0:T(8,128)(2,1)S(1)} %all_to_all.17.refs_0_), channel_id=1, source_target_pairs={{0,2},{2,0},{4,6},{6,4},{8,10},{10,8},{12,14},{14,12},{16,18},{18,... | collective-permute-start | bytes 3145736 | tf_op jit(solution)/shard_map/ppermute | solution.py:354
  118.1 1.0 copy-start.3
  122.4 6.5 %collective-permute-start.4 = (f32[256,128]{1,0:T(8,128)}, f32[256,128]{1,0:T(8,128)S(1)}, u32[]{:S(2)}, u32[]{:S(2)}) collective-permute-start(f32[256,128]{1,0:T(8,128)} %project_other.1), channel_id=1, source_target_pairs={{0,1},{1,0},{2,3},{3,2},{4,5},{5,4},{6,7},{7,6},{8,9},{9,8},{10,11... | collective-permute-start | bytes 393224 | tf_op jit(solution)/shard_map/ppermute | solution.py:370

commit v2 on v1

--- a/solution.py
+++ b/solution.py
@@ -26,6 +26,8 @@
 SAME_CORE = [[2 * i + c for i in range(CHIPS)] for c in range(2)]
 CORE_SWAP = [(i, i ^ 1) for i in range(REQS)]
 
+LIMIT = pltpu.CompilerParams(vmem_limit_bytes=24 << 20)
+
 VM = pl.BlockSpec(memory_space=pltpu.VMEM)
 SM = pl.BlockSpec(memory_space=pltpu.SMEM)
 HB = pl.BlockSpec(memory_space=pl.ANY)
@@ -43,10 +45,11 @@
     return lax.broadcasted_iota(jnp.int32, shape, dim)
 
 
-def pack_kernel(mem_ref, q_ref, out_ref, tmp):
+def pack_kernel(mem_ref, q_ref, out_ref, own_ref, tmp):
     for head in range(32):
         tmp[pl.ds(head * STEPS, STEPS), :] = q_ref[0, :, pl.ds(head * HEAD, HEAD)].astype(F32)
     data = tmp[...].astype(BF)
+    own_ref[...] = data
     side = jnp.full((8, HEAD), mem_ref[0, 0], jnp.int32).astype(F32).astype(BF)
     for i in range(CHIPS):
         out_ref[i, pl.ds(0, 128), :] = data
@@ -56,10 +59,14 @@
 def pack(membership, queries):
     return pl.pallas_call(
         pack_kernel,
-        out_shape=jax.ShapeDtypeStruct((CHIPS, PAY, HEAD), BF),
+        out_shape=[
+            jax.ShapeDtypeStruct((CHIPS, PAY, HEAD), BF),
+            jax.ShapeDtypeStruct((128, HEAD), BF),
+        ],
         in_specs=[SM, VM],
-        out_specs=VM,
+        out_specs=[VM, VM],
         scratch_shapes=[pltpu.VMEM((128, HEAD), F32)],
+        compiler_params=LIMIT,
         name="pack",
     )(membership, queries)
 
@@ -80,7 +87,7 @@
         hot_hi = jnp.where(sub_hi == lax.shift_right_logical(pos, 7), 1.0, 0.0).astype(BF)
         hot_lo = jnp.where(sub_lo == (pos & 127), 1.0, 0.0).astype(BF)
         count = nt(hot_hi, hot_lo)
-        q = q_ref[0, pl.ds(g * ROWS, ROWS), :]
+        q = q_ref[pl.ds(g * ROWS, ROWS), :]
         s = nt(q, hk_ref[0, :, lanes])
         s = jnp.concatenate(
             [
@@ -102,7 +109,7 @@
         l_ref[g] = peak * C2 + jnp.log(total) * LOG2E
 
 
-def private(packed, kept, hk, hv, nk, nv):
+def private(own, kept, hk, hv, nk, nv):
     return pl.pallas_call(
         private_kernel,
         out_shape=[jax.ShapeDtypeStruct((4, ROWS, HEAD), F32)] * 2,
@@ -112,8 +119,9 @@
         cost_estimate=pl.CostEstimate(
             flops=400_000_000, transcendentals=300_000, bytes_accessed=5_000_000
         ),
+        compiler_params=LIMIT,
         name="private",
-    )(packed[:1], kept, hk, hv, nk, nv)
+    )(own, kept, hk, hv, nk, nv)
 
 
 def prefix_kernel(
@@ -239,6 +247,7 @@
         cost_estimate=pl.CostEstimate(
             flops=600_000_000, transcendentals=1_000_000, bytes_accessed=6_000_000
         ),
+        compiler_params=LIMIT,
         name="prefix_keep" if keep else "prefix_send",
     )(qa, qb, k, v, po, pll)
 
@@ -271,6 +280,7 @@
         out_shape=jax.ShapeDtypeStruct((CHIPS, PAY, HEAD), BF),
         in_specs=[VM] * 4,
         out_specs=VM,
+        compiler_params=LIMIT,
         name="merge",
     )(o1, l1, o2, l2)
 
@@ -301,6 +311,7 @@
         in_specs=[VM],
         out_specs=VM,
         scratch_shapes=[pltpu.VMEM((128, HEAD), F32)],
+        compiler_params=LIMIT,
         name="combine",
     )(x)
 
@@ -340,6 +351,7 @@
         cost_estimate=pl.CostEstimate(
             flops=140_000_000, transcendentals=0, bytes_accessed=2_000_000
         ),
+        compiler_params=LIMIT,
         name="project_own" if own else "project_other",
     )(a, w, *base)
 
@@ -355,10 +367,11 @@
 
 
 def local(queries, nk, nv, pk, pv, hk, hv, kept, membership, out_weight):
-    packed = pack(membership, queries)
+    packed, own = pack(membership, queries)
     qa = over_chips(packed)
+    po, pll = private(own, kept, hk, hv, nk, nv)
+    qa, po, pll = lax.optimization_barrier((qa, po, pll))
     qb = swap_cores(qa)
-    po, pll = private(packed, kept, hk, hv, nk, nv)
     send_o, send_l = prefix(False, qa, qb, pk, pv, po, pll)
     got_o, got_l = swap_cores(send_o), swap_cores(send_l)
     keep_o, keep_l = prefix(True, qa, qb, pk, pv, po, pll)

time: 132 us -> 105 us (0.80)
  blocking collectives: 68.9 us -> 40 us
  Pallas kernels: 43.2 us -> 21.2 us
  waiting for transfers between devices: 3.13 us -> 17.6 us
  starting transfers between devices: 8.54 us -> 18.7 us
    all_to_all x3 -> x2, blocking collectives: 68.9 us -> 40 us  [over_chips(): lax.all_to_all(x, 'req', split_axis=0, concat_axis=0, axis_index_groups=S...]
    all_to_all x0 -> x1, waiting for transfers between devices: none -> 9.86 us  [over_chips(): lax.all_to_all(x, 'req', split_axis=0, concat_axis=0, axis_index_groups=S...]
    all_to_all x0 -> x1, starting transfers between devices: none -> 9.21 us  [over_chips(): lax.all_to_all(x, 'req', split_axis=0, concat_axis=0, axis_index_groups=S...]
    pallas_call x2, Pallas kernels: 22.1 us -> 14.7 us  [prefix(): pl.pallas_call(functools.partial(prefix_kernel, keep), out_shape=[jax.Sha...]
    pallas_call x2, Pallas kernels: 6.69 us -> 0.95 us  [project(): pl.pallas_call(functools.partial(project_kernel, own), out_shape=jax.Shap...]
    ppermute x4, waiting for transfers between devices: 0.01 us -> 4.19 us  [swap_cores(): return lax.ppermute(x, 'req', CORE_SWAP)]
    pallas_call x1, Pallas kernels: 5.66 us -> 2.75 us  [private(): pl.pallas_call(private_kernel, out_shape=[jax.ShapeDtypeStruct((4, ROWS,...]
    pallas_call x1, Pallas kernels: 3.65 us -> 0.79 us  [merge(): pl.pallas_call(merge_kernel, out_shape=jax.ShapeDtypeStruct((CHIPS, PAY,...]
  transfers between devices with their start and end apart: 5 -> 6, of which waited for: 1 -> 4; matrix products, arithmetic and copies ran while one was open for 1% -> 0% of each run, Pallas kernels for 16% -> 10%
where the time goes in v2:
time: 105 us; the launch traced here: 104 us
  blocking collectives  40 us (38%)
  Pallas kernels  21.2 us (20%)
  starting transfers between devices  18.7 us (18%)
  waiting for transfers between devices  17.6 us (17%)
  local copies, waits for them, and re-layouts  5.54 us (5%)
    all_to_all x2, blocking collectives, over_chips(): lax.all_to_all(x, 'req', split_axis=0, concat_axis=0, axis_index_groups=S...  40 us
    pallas_call x2, Pallas kernels, prefix(): pl.pallas_call(functools.partial(prefix_kernel, keep), out_shape=[jax.Sha...  14.7 us
    all_to_all x1, waiting for transfers between devices, over_chips(): lax.all_to_all(x, 'req', split_axis=0, concat_axis=0, axis_index_groups=S...  9.86 us
    all_to_all x1, starting transfers between devices, over_chips(): lax.all_to_all(x, 'req', split_axis=0, concat_axis=0, axis_index_groups=S...  9.21 us
    ppermute x4, starting transfers between devices, swap_cores(): return lax.ppermute(x, 'req', CORE_SWAP)  6.08 us
    unnamed x18, local copies, waits for them, and re-layouts  5.54 us
    ppermute x4, waiting for transfers between devices, swap_cores(): return lax.ppermute(x, 'req', CORE_SWAP)  4.19 us
    ppermute x1, waiting for transfers between devices, local(): theirs = lax.ppermute(mine, 'kvh', [(0, 1), (1, 0)])  3.5 us
  transfers between devices with their start and end apart: 6, of which 4 were waited for; matrix products, arithmetic and copies ran while one was open for 0% of the time, Pallas kernels for 10%

profile of v2, /device:TPU:1, one launch (start us, length us, event | category | flops | bytes accessed | tf_op | source)
XLA Modules:
  0.0 104.5 jit_solution(15992999725526417592)
XLA Ops:
  0.7 0.0 copy-start.5
  0.7 0.7 copy-done.5
  1.4 1.1 %pack.1 = (bf16[32,136,128]{2,1,0:T(8,128)(2,1)}, bf16[128,128]{1,0:T(8,128)(2,1)S(1)}) custom-call(s32[1,1]{1,0:T(1,128)S(6)} %copy.11.mem_ref, bf16[1,4,4096]{2,1,0:T(4,128)(2,1)S(1)} %copy-done.5), custom_call_target="tpu_custom_call" | custom-call | tf_op jit(solution)/shard_map/pack/pallas_call | solution.py:60
  2.5 9.2 %all-to-all-start = ((bf16[32,136,128]{2,1,0:T(8,128)(2,1)}), bf16[32,136,128]{2,1,0:T(8,128)(2,1)S(1)}, u32[]{:S(2)}, u32[]{:S(2)}) async-start(bf16[32,136,128]{2,1,0:T(8,128)(2,1)} %get-tuple-element.16), calls=%async_computation | async-start | bytes 2228224 | tf_op jit(solution)/shard_map/all_to_all | solution.py:360
  11.7 0.0 copy-done.6
  11.7 0.0 copy-done.7
  11.8 0.0 copy-start.3
  11.8 1.6 %copy-done.3 = bf16[1,2048,512]{2,1,0:T(8,128)(2,1)S(1)} copy-done((bf16[1,2048,512]{2,1,0:T(8,128)(2,1)S(1)}, bf16[1,2048,512]{2,1,0:T(8,128)(2,1)}, u32[]{:S(2)}) %copy-start.3) | copy-done | bytes 2097176
  13.4 1.6 %copy-done.4 = bf16[1,2048,512]{2,1,0:T(8,128)(2,1)S(1)} copy-done((bf16[1,2048,512]{2,1,0:T(8,128)(2,1)S(1)}, bf16[1,2048,512]{2,1,0:T(8,128)(2,1)}, u32[]{:S(2)}) %copy-start.4) | copy-done | bytes 2097176
  14.9 2.7 %private.1 = (f32[4,32,128]{2,1,0:T(8,128)S(1)}, f32[4,32,128]{2,1,0:T(8,128)S(1)}) custom-call(bf16[128,128]{1,0:T(8,128)(2,1)S(1)} %get-tuple-element.17.q_ref, s32[1,4,1024]{2,1,0:T(4,128)S(1)} %copy-done.6, bf16[1,2048,512]{2,1,0:T(8,128)(2,1)S(1)} %copy-done.3, bf16[1,2048,512]{2,1,0:T(8,128)(2,1)S(1)} %copy-done.4, bf16[1,4,512]{2,1,0:T(4,128)(2,1)S(1)} %copy-done.7, ...), custom_call_target="tpu_custom_call" | custom-call | flops 400000000 | bytes 5000000 | tf_op jit(solution)/shard_map/private/pallas_call | solution.py:113
  17.7 9.9 %all-to-all-done.qa_hbm = bf16[32,136,128]{2,1,0:T(8,128)(2,1)S(1)} async-done(((bf16[32,136,128]{2,1,0:T(8,128)(2,1)}), bf16[32,136,128]{2,1,0:T(8,128)(2,1)S(1)}, u32[]{:S(2)}, u32[]{:S(2)}) %all-to-all-start) | async-done | bytes 1114144 | tf_op jit(solution)/shard_map/all_to_all | solution.py:360
  27.6 2.4 %collective-permute-start = (bf16[32,136,128]{2,1,0:T(8,128)(2,1)S(1)}, bf16[32,136,128]{2,1,0:T(8,128)(2,1)S(1)}, u32[]{:S(2)}, u32[]{:S(2)}) collective-permute-start(bf16[32,136,128]{2,1,0:T(8,128)(2,1)S(1)} %all-to-all-done.qa_hbm), channel_id=1, source_target_pairs={{0,2},{2,0},{4,6},{6,4},{8,10},{10,8},{12,14},{14,12},{16,18},{18,... | collective-permute-start | bytes 3342344 | tf_op jit(solution)/shard_map/ppermute | solution.py:366
  29.9 2.4 %collective-permute-done.qb_hbm = bf16[32,136,128]{2,1,0:T(8,128)(2,1)S(1)} collective-permute-done((bf16[32,136,128]{2,1,0:T(8,128)(2,1)S(1)}, bf16[32,136,128]{2,1,0:T(8,128)(2,1)S(1)}, u32[]{:S(2)}, u32[]{:S(2)}) %collective-permute-start) | collective-permute-done | bytes 1114144 | tf_op jit(solution)/shard_map/ppermute | solution.py:366
  32.3 1.6 %copy-done.1 = bf16[8,256,512]{2,1,0:T(8,128)(2,1)S(1)} copy-done((bf16[8,256,512]{2,1,0:T(8,128)(2,1)S(1)}, bf16[8,256,512]{2,1,0:T(8,128)(2,1)}, u32[]{:S(2)}) %copy-start.1) | copy-done | bytes 2097176
  33.9 7.2 %prefix_send.1 = (bf16[32,128,128]{2,1,0:T(8,128)(2,1)S(1)}, f32[32,128]{1,0:T(8,128)S(1)}) custom-call(bf16[32,136,128]{2,1,0:T(8,128)(2,1)S(1)} %all-to-all-done.qa_hbm, bf16[32,136,128]{2,1,0:T(8,128)(2,1)S(1)} %collective-permute-done.qb_hbm, bf16[8,256,512]{2,1,0:T(8,128)(2,1)S(1)} %copy-done, bf16[8,256,512]{2,1,0:T(8,128)(2,1)S(1)} %copy-done.1, ...), custom_call_target="tpu_custom_call" | custom-call | flops 600000000 | bytes 6000000 | tf_op jit(solution)/shard_map/prefix_send/pallas_call | solution.py:227
  41.1 0.5 collective-permute-start.1
  41.6 0.1 collective-permute-start.2
  41.7 7.4 %prefix_keep.1 = (f32[32,128,128]{2,1,0:T(8,128)S(1)}, f32[32,128]{1,0:T(8,128)S(1)}) custom-call(bf16[32,136,128]{2,1,0:T(8,128)(2,1)S(1)} %all-to-all-done.qa_hbm, bf16[32,136,128]{2,1,0:T(8,128)(2,1)S(1)} %collective-permute-done.qb_hbm, bf16[8,256,512]{2,1,0:T(8,128)(2,1)S(1)} %copy-done, bf16[8,256,512]{2,1,0:T(8,128)(2,1)S(1)} %copy-done.1, ...), custom_call_target="tpu_custom_call" | custom-call | flops 600000000 | bytes 6000000 | tf_op jit(solution)/shard_map/prefix_keep/pallas_call | solution.py:227
  49.2 0.0 collective-permute-done.2.l2_ref
  49.2 0.0 collective-permute-done.1.o2_ref
  49.2 0.8 merge.1
  50.0 22.5 %all_to_all.15.in_ref = bf16[32,136,128]{2,1,0:T(8,128)(2,1)S(1)} all-to-all(bf16[32,136,128]{2,1,0:T(8,128)(2,1)S(1)} %merge.1), channel_id=1, replica_groups={{0,4,8,12,16,20,24,28,32,36,40,44,48,52,56,60,64,68,72,76,80,84,88,92,9..., dimensions={0} | all-to-all | bytes 2228224 | tf_op jit(solution)/shard_map/all_to_all | solution.py:360
  72.5 1.0 combine.1
  73.5 17.5 %all_to_all.16.refs_0_ = bf16[32,128,128]{2,1,0:T(8,128)(2,1)S(1)} all-to-all(bf16[32,128,128]{2,1,0:T(8,128)(2,1)S(1)} %combine.1), channel_id=1, replica_groups={{0,4,8,12,16,20,24,28,32,36,40,44,48,52,56,60,64,68,72,76,80,84,88,92,9..., dimensions={0} | all-to-all | bytes 2097152 | tf_op jit(solution)/shard_map/all_to_all | solution.py:360
  91.0 3.1 %collective-permute-start.3 = (bf16[32,128,128]{2,1,0:T(8,128)(2,1)S(1)}, bf16[32,128,128]{2,1,0:T(8,128)(2,1)S(1)}, u32[]{:S(2)}, u32[]{:S(2)}) collective-permute-start(bf16[32,128,128]{2,1,0:T(8,128)(2,1)S(1)} %all_to_all.16.refs_0_), channel_id=1, source_target_pairs={{0,2},{2,0},{4,6},{6,4},{8,10},{10,8},{12,14},{14,12},{16,18},{18,... | collective-permute-start | bytes 3145736 | tf_op jit(solution)/shard_map/ppermute | solution.py:366
  94.1 0.0 copy-done.2
  94.2 0.5 project_own.1.refs_2_
  94.6 1.8 %collective-permute-done.3.refs_0_ = bf16[32,128,128]{2,1,0:T(8,128)(2,1)S(1)} collective-permute-done((bf16[32,128,128]{2,1,0:T(8,128)(2,1)S(1)}, bf16[32,128,128]{2,1,0:T(8,128)(2,1)S(1)}, u32[]{:S(2)}, u32[]{:S(2)}) %collective-permute-start.3) | collective-permute-done | bytes 1048608 | tf_op jit(solution)/shard_map/ppermute | solution.py:366
  96.4 0.5 project_other.1
  96.9 3.4 %collective-permute-start.4 = (f32[256,128]{1,0:T(8,128)S(1)}, f32[256,128]{1,0:T(8,128)S(1)}, u32[]{:S(2)}, u32[]{:S(2)}) collective-permute-start(f32[256,128]{1,0:T(8,128)S(1)} %project_other.1), channel_id=1, source_target_pairs={{0,1},{1,0},{2,3},{3,2},{4,5},{5,4},{6,7},{7,6},{8,9},{9,8},{10,11... | collective-permute-start | bytes 393224 | tf_op jit(solution)/shard_map/ppermute | solution.py:383
  100.3 3.5 %collective-permute-done.4 = f32[256,128]{1,0:T(8,128)S(1)} collective-permute-done((f32[256,128]{1,0:T(8,128)S(1)}, f32[256,128]{1,0:T(8,128)S(1)}, u32[]{:S(2)}, u32[]{:S(2)}) %collective-permute-start.4) | collective-permute-done | bytes 131104 | tf_op jit(solution)/shard_map/ppermute | solution.py:383
  103.8 0.7 add_convert_fusion
  (9 shorter events, 0.0 us)
Async XLA Ops:
  0.7 0.8 copy-start.5
  1.4 10.3 %copy-start.6 = (s32[1,4,1024]{2,1,0:T(4,128)S(1)}, s32[1,4,1024]{2,1,0:T(4,128)}, u32[]{:S(2)}) copy-start(s32[1,4,1024]{2,1,0:T(4,128)} %kept_ref.1) | copy-start | bytes 49156
  1.4 10.3 %copy-start.7 = (bf16[1,4,512]{2,1,0:T(4,128)(2,1)S(1)}, bf16[1,4,512]{2,1,0:T(4,128)(2,1)}, u32[]{:S(2)}) copy-start(bf16[1,4,512]{2,1,0:T(4,128)(2,1)} %nk_ref.1) | copy-start | bytes 12292
  1.4 10.3 %copy-start.8 = (bf16[1,4,512]{2,1,0:T(4,128)(2,1)S(1)}, bf16[1,4,512]{2,1,0:T(4,128)(2,1)}, u32[]{:S(2)}) copy-start(bf16[1,4,512]{2,1,0:T(4,128)(2,1)} %nv_ref.1) | copy-start | bytes 12292
  2.5 25.1 %all-to-all-start = ((bf16[32,136,128]{2,1,0:T(8,128)(2,1)}), bf16[32,136,128]{2,1,0:T(8,128)(2,1)S(1)}, u32[]{:S(2)}, u32[]{:S(2)}) async-start(bf16[32,136,128]{2,1,0:T(8,128)(2,1)} %get-tuple-element.16), calls=%async_computation | async-start | bytes 2228224 | tf_op jit(solution)/shard_map/all_to_all | solution.py:360
  11.8 1.6 %copy-start.3 = (bf16[1,2048,512]{2,1,0:T(8,128)(2,1)S(1)}, bf16[1,2048,512]{2,1,0:T(8,128)(2,1)}, u32[]{:S(2)}) copy-start(bf16[1,2048,512]{2,1,0:T(8,128)(2,1)} %hk_ref.1) | copy-start | bytes 6291460
  13.4 1.6 %copy-start.4 = (bf16[1,2048,512]{2,1,0:T(8,128)(2,1)S(1)}, bf16[1,2048,512]{2,1,0:T(8,128)(2,1)}, u32[]{:S(2)}) copy-start(bf16[1,2048,512]{2,1,0:T(8,128)(2,1)} %hv_ref.1) | copy-start | bytes 6291460
  14.9 17.4 %copy-start = (bf16[8,256,512]{2,1,0:T(8,128)(2,1)S(1)}, bf16[8,256,512]{2,1,0:T(8,128)(2,1)}, u32[]{:S(2)}) copy-start(bf16[8,256,512]{2,1,0:T(8,128)(2,1)} %k_hbm.3) | copy-start | bytes 6291460
  27.6 4.7 %collective-permute-start = (bf16[32,136,128]{2,1,0:T(8,128)(2,1)S(1)}, bf16[32,136,128]{2,1,0:T(8,128)(2,1)S(1)}, u32[]{:S(2)}, u32[]{:S(2)}) collective-permute-start(bf16[32,136,128]{2,1,0:T(8,128)(2,1)S(1)} %all-to-all-done.qa_hbm), channel_id=1, source_target_pairs={{0,2},{2,0},{4,6},{6,4},{8,10},{10,8},{12,14},{14,12},{16,18},{18,... | collective-permute-start | bytes 3342344 | tf_op jit(solution)/shard_map/ppermute | solution.py:366
  32.3 1.6 %copy-start.1 = (bf16[8,256,512]{2,1,0:T(8,128)(2,1)S(1)}, bf16[8,256,512]{2,1,0:T(8,128)(2,1)}, u32[]{:S(2)}) copy-start(bf16[8,256,512]{2,1,0:T(8,128)(2,1)} %v_hbm.3) | copy-start | bytes 6291460
  41.1 8.0 %collective-permute-start.1 = (bf16[32,128,128]{2,1,0:T(8,128)(2,1)S(1)}, bf16[32,128,128]{2,1,0:T(8,128)(2,1)S(1)}, u32[]{:S(2)}, u32[]{:S(2)}) collective-permute-start(bf16[32,128,128]{2,1,0:T(8,128)(2,1)S(1)} %get-tuple-element.25), channel_id=1, source_target_pairs={{0,2},{2,0},{4,6},{6,4},{8,10},{10,8},{12,14},{14,12},{16,18},{18,... | collective-permute-start | bytes 3145736 | tf_op jit(solution)/shard_map/ppermute | solution.py:366
  41.6 7.6 %collective-permute-start.2 = (f32[32,128]{1,0:T(8,128)S(1)}, f32[32,128]{1,0:T(8,128)S(1)}, u32[]{:S(2)}, u32[]{:S(2)}) collective-permute-start(f32[32,128]{1,0:T(8,128)S(1)} %get-tuple-element.26), channel_id=1, source_target_pairs={{0,2},{2,0},{4,6},{6,4},{8,10},{10,8},{12,14},{14,12},{16,18},{18,... | collective-permute-start | bytes 49160 | tf_op jit(solution)/shard_map/ppermute | solution.py:366
  72.5 21.6 %copy-start.2 = (bf16[4096,128]{1,0:T(8,128)(2,1)S(1)}, bf16[4096,128]{1,0:T(8,128)(2,1)}, u32[]{:S(2)}) copy-start(bf16[4096,128]{1,0:T(8,128)(2,1)} %refs_1_.3) | copy-start | bytes 3145732
  91.0 5.4 %collective-permute-start.3 = (bf16[32,128,128]{2,1,0:T(8,128)(2,1)S(1)}, bf16[32,128,128]{2,1,0:T(8,128)(2,1)S(1)}, u32[]{:S(2)}, u32[]{:S(2)}) collective-permute-start(bf16[32,128,128]{2,1,0:T(8,128)(2,1)S(1)} %all_to_all.16.refs_0_), channel_id=1, source_target_pairs={{0,2},{2,0},{4,6},{6,4},{8,10},{10,8},{12,14},{14,12},{16,18},{18,... | collective-permute-start | bytes 3145736 | tf_op jit(solution)/shard_map/ppermute | solution.py:366
  96.9 6.9 %collective-permute-start.4 = (f32[256,128]{1,0:T(8,128)S(1)}, f32[256,128]{1,0:T(8,128)S(1)}, u32[]{:S(2)}, u32[]{:S(2)}) collective-permute-start(f32[256,128]{1,0:T(8,128)S(1)} %project_other.1), channel_id=1, source_target_pairs={{0,1},{1,0},{2,3},{3,2},{4,5},{5,4},{6,7},{7,6},{8,9},{9,8},{10,11... | collective-permute-start | bytes 393224 | tf_op jit(solution)/shard_map/ppermute | solution.py:383

commit v3 on v1

v3 whole, which is shorter than its diff:
```python
import jax
import jax.numpy as jnp
from jax import lax
from jax.experimental import pallas as pl
from jax.experimental.pallas import tpu as pltpu
from jax.sharding import PartitionSpec as P

HEAD = 128
PROMPTS = 8
STEPS = 4
ROWS = 32
REQS = 64
CHIPS = 32
PORTION = 256
HISTORY = 2048
KEPT = 1024
GROUP = 4
PAY = 136
LOG2E = 1.4426950408889634
C2 = HEAD ** -0.5 * LOG2E
NEG = -1e30
BF = jnp.bfloat16
F32 = jnp.float32

SAME_CORE = [[2 * i + c for i in range(CHIPS)] for c in range(2)]
CORE_SWAP = [(i, i ^ 1) for i in range(REQS)]

LIMIT = pltpu.CompilerParams(vmem_limit_bytes=24 << 20)

VM = pl.BlockSpec(memory_space=pltpu.VMEM)
SM = pl.BlockSpec(memory_space=pltpu.SMEM)
HB = pl.BlockSpec(memory_space=pltpu.HBM)


def in_hbm(x):
    return pltpu.with_memory_space_constraint(x, pltpu.HBM)


def nt(a, b):
    return lax.dot_general(a, b, (((1,), (1,)), ((), ())), preferred_element_type=F32)


def mm(a, b):
    return lax.dot_general(a, b, (((1,), (0,)), ((), ())), preferred_element_type=F32)


def iota(shape, dim):
    return lax.broadcasted_iota(jnp.int32, shape, dim)


def spread(tile, out_ref, sem):
    copies = [pltpu.make_async_copy(tile, out_ref.at[i], sem.at[i]) for i in range(CHIPS)]
    for copy in copies:
        copy.start()
    for copy in copies:
        copy.wait()


def pack_kernel(mem_ref, q_ref, out_ref, own_ref, tmp, tile, sem):
    for head in range(32):
        tmp[pl.ds(head * STEPS, STEPS), :] = q_ref[0, :, pl.ds(head * HEAD, HEAD)].astype(F32)
    data = tmp[...].astype(BF)
    own_ref[...] = data
    side = jnp.full((8, HEAD), mem_ref[0, 0], jnp.int32).astype(F32).astype(BF)
    tile[pl.ds(0, 128), :] = data
    tile[pl.ds(128, 8), :] = side
    spread(tile, out_ref, sem)


def pack(membership, queries):
    return pl.pallas_call(
        pack_kernel,
        out_shape=[
            pltpu.HBM((CHIPS, PAY, HEAD), BF),
            jax.ShapeDtypeStruct((128, HEAD), BF),
        ],
        in_specs=[SM, VM],
        out_specs=[HB, VM],
        scratch_shapes=[
            pltpu.VMEM((128, HEAD), F32),
            pltpu.VMEM((PAY, HEAD), BF),
            pltpu.SemaphoreType.DMA((CHIPS,)),
        ],
        compiler_params=LIMIT,
        name="pack",
    )(membership, queries)


def private_kernel(q_ref, kept_ref, hk_ref, hv_ref, nk_ref, nv_ref, o_ref, l_ref, knew, vnew):
    ones = jnp.ones((HISTORY, HEAD), BF)
    ones_new = jnp.ones((128, HEAD), BF)
    sub_hi = iota((16, KEPT), 0)
    sub_lo = iota((128, KEPT), 0)
    col = iota((ROWS, 128), 1)
    step_of = iota((ROWS, 128), 0) & (STEPS - 1)
    new_ok = (col < STEPS) & (col <= step_of)
    knew[...] = jnp.zeros_like(knew)
    vnew[...] = jnp.zeros_like(vnew)
    for g in range(4):
        lanes = pl.ds(g * HEAD, HEAD)
        pos = kept_ref[0, pl.ds(g, 1), :]
        hot_hi = jnp.where(sub_hi == lax.shift_right_logical(pos, 7), 1.0, 0.0).astype(BF)
        hot_lo = jnp.where(sub_lo == (pos & 127), 1.0, 0.0).astype(BF)
        count = nt(hot_hi, hot_lo)
        q = q_ref[pl.ds(g * ROWS, ROWS), :]
        s = nt(q, hk_ref[0, :, lanes])
        s = jnp.concatenate(
            [
                jnp.where(count[i : i + 1, :] > 0.5, s[:, i * 128 : (i + 1) * 128], NEG)
                for i in range(16)
            ],
            axis=1,
        )
        knew[pl.ds(0, STEPS), :] = nk_ref[0, :, lanes].astype(F32)
        vnew[pl.ds(0, STEPS), :] = nv_ref[0, :, lanes].astype(F32)
        sn = jnp.where(new_ok, nt(q, knew[...].astype(BF)), NEG)
        peak = jnp.maximum(jnp.max(s, axis=1, keepdims=True), jnp.max(sn, axis=1, keepdims=True))
        p = jnp.exp2((s - peak) * C2).astype(BF)
        pn = jnp.exp2((sn - peak) * C2).astype(BF)
        ov = mm(p, jnp.concatenate([hv_ref[0, :, lanes], ones], axis=1))
        ov += mm(pn, jnp.concatenate([vnew[...].astype(BF), ones_new], axis=1))
        total = ov[:, HEAD:]
        o_ref[g] = ov[:, :HEAD] / total
        l_ref[g] = peak * C2 + jnp.log(total) * LOG2E


def private(own, kept, hk, hv, nk, nv):
    return pl.pallas_call(
        private_kernel,
        out_shape=[jax.ShapeDtypeStruct((4, ROWS, HEAD), F32)] * 2,
        in_specs=[VM] * 6,
        out_specs=[VM] * 2,
        scratch_shapes=[pltpu.VMEM((128, HEAD), F32)] * 2,
        cost_estimate=pl.CostEstimate(
            flops=400_000_000, transcendentals=300_000, bytes_accessed=5_000_000
        ),
        compiler_params=LIMIT,
        name="private",
    )(own, kept, hk, hv, nk, nv)


def prefix_kernel(q, k0h, v0h, k1h, v1h, out_ref, k0, v0, k1, v1, lbuf, tab_v, tab_s, tsem, ksem):
    def fetch(p):
        pairs = ((k0h, k0), (v0h, v0), (k1h, k1), (v1h, v1))
        return [pltpu.make_async_copy(a.at[p], b.at[p], ksem.at[p, i]) for i, (a, b) in enumerate(pairs)]

    for p in range(PROMPTS):
        for copy in fetch(p):
            copy.start()

    sides = q[:, pl.ds(128, 8), :].astype(F32)
    member = jnp.max(sides, axis=1)
    member = jnp.concatenate([member, jnp.full((96, HEAD), 99.0, F32)], axis=0)
    across = member.T
    row, lane = iota((128, 128), 0), iota((128, 128), 1)
    before = (across < member) | ((across == member) & (lane < row))
    slot = jnp.sum(jnp.where(before, 1.0, 0.0), axis=1, keepdims=True)
    lanef = lane.astype(F32)
    here = slot == jnp.minimum(lanef, CHIPS - 1.0)

    def total(x):
        return jnp.sum(x, axis=0, keepdims=True)

    order = total(jnp.where(here, row.astype(F32), 0.0))
    starts = total(jnp.where(member < lanef, 1.0, 0.0))
    counts = total(jnp.where(member == lanef, 1.0, 0.0))
    table = jnp.concatenate([order, starts, counts, jnp.zeros((5, 128), F32)], axis=0)
    tab_v[...] = table.astype(jnp.int32)
    ct = pltpu.make_async_copy(tab_v, tab_s, tsem)
    ct.start()
    ct.wait()

    ones = jnp.ones((PORTION, HEAD), BF)

    def prompt(p, carry):
        for copy in fetch(p):
            copy.wait()
        start = tab_s[1, p]
        chunks = (tab_s[2, p] + GROUP - 1) // GROUP

        def chunk(i, c):
            slot0 = start + i * GROUP
            at = [tab_s[0, slot0 + j] for j in range(GROUP)]
            for g in range(4):
                rows, lanes = pl.ds(g * ROWS, ROWS), pl.ds(g * HEAD, HEAD)
                qs = jnp.concatenate([q[t, rows, :] for t in at], axis=0)
                s0 = nt(qs, k0[p, :, lanes])
                s1 = nt(qs, k1[p, :, lanes])
                peak = jnp.maximum(jnp.max(s0, axis=1, keepdims=True), jnp.max(s1, axis=1, keepdims=True))
                w0 = jnp.exp2((s0 - peak) * C2).astype(BF)
                w1 = jnp.exp2((s1 - peak) * C2).astype(BF)
                ov = mm(w0, jnp.concatenate([v0[p, :, lanes], ones], axis=1))
                ov += mm(w1, jnp.concatenate([v1[p, :, lanes], ones], axis=1))
                l = ov[:, HEAD:]
                o = (ov[:, :HEAD] / l).astype(BF)
                lse = peak * C2 + jnp.log(l) * LOG2E
                for j in reversed(range(GROUP)):
                    out_ref[at[j], rows, :] = o[j * ROWS : (j + 1) * ROWS]
                    lbuf[at[j], rows, :] = lse[j * ROWS : (j + 1) * ROWS]
            return c

        return lax.fori_loop(0, chunks, chunk, carry)

    lax.fori_loop(0, PROMPTS, prompt, 0)

    diag = row == lane
    sub = iota((8, 128), 0)
    for n in range(CHIPS):
        lse = total(jnp.where(diag, lbuf[n], 0.0))
        hi = lse.astype(BF).astype(F32)
        mid = (lse - hi).astype(BF).astype(F32)
        lo = lse - hi - mid
        side = jnp.where(sub == 0, hi, jnp.where(sub == 1, mid, jnp.where(sub == 2, lo, 0.0)))
        out_ref[n, pl.ds(128, 8), :] = side.astype(BF)


def prefix(q, k0, v0, k1, v1):
    return pl.pallas_call(
        prefix_kernel,
        out_shape=jax.ShapeDtypeStruct((CHIPS, PAY, HEAD), BF),
        in_specs=[VM] + [HB] * 4,
        out_specs=VM,
        scratch_shapes=[pltpu.VMEM((PROMPTS, PORTION, 512), BF)] * 4
        + [
            pltpu.VMEM((CHIPS, 128, HEAD), F32),
            pltpu.VMEM((8, 128), jnp.int32),
            pltpu.SMEM((8, 128), jnp.int32),
            pltpu.SemaphoreType.DMA(()),
            pltpu.SemaphoreType.DMA((PROMPTS, 4)),
        ],
        compiler_params=LIMIT,
        cost_estimate=pl.CostEstimate(
            flops=1_200_000_000, transcendentals=2_000_000, bytes_accessed=10_000_000
        ),
        name="prefix",
    )(q, in_hbm(k0), in_hbm(v0), k1, v1)


def combine_kernel(in_ref, po_ref, pl_ref, out_ref, tile, sem):
    row, lane = iota((128, 128), 0), iota((128, 128), 1)
    own = jnp.sum(jnp.where(row == lane, pl_ref[...].reshape(128, 128), 0.0), axis=0, keepdims=True)
    pieces = [in_ref[n, pl.ds(128, 8), :].astype(F32) for n in range(CHIPS)]
    lse = jnp.concatenate([x[0:1] + x[1:2] + x[2:3] for x in pieces], axis=0)
    top = jnp.maximum(jnp.max(lse, axis=0, keepdims=True), own)
    e, eo = jnp.exp2(lse - top), jnp.exp2(own - top)
    both = jnp.sum(e, axis=0, keepdims=True) + eo
    cols = jnp.concatenate([e / both, jnp.zeros((95, 128), F32), eo / both], axis=0).T
    acc = cols[:, 127:128] * po_ref[...].reshape(128, HEAD)
    for n in range(CHIPS):
        acc += cols[:, n : n + 1] * in_ref[n, pl.ds(0, 128), :].astype(F32)
    sub = iota((8, 128), 0)
    tiles = []
    for j in range(16):
        g, h = j // 8, j % 8
        a = acc[g * ROWS + h // 2 * 8 : g * ROWS + h // 2 * 8 + 8]
        b = acc[(g + 2) * ROWS + h // 2 * 8 : (g + 2) * ROWS + h // 2 * 8 + 8]
        if h % 2 == 0:
            tiles.append(jnp.where(sub < STEPS, a, pltpu.roll(b, STEPS, 0)))
        else:
            tiles.append(jnp.where(sub < STEPS, pltpu.roll(a, STEPS, 0), b))
    tile[...] = jnp.concatenate(tiles, axis=1).astype(BF)
    spread(tile, out_ref, sem)


def combine(x, po, pll):
    return pl.pallas_call(
        combine_kernel,
        out_shape=jax.ShapeDtypeStruct((CHIPS, 8, 2048), BF),
        in_specs=[VM] * 3,
        out_specs=HB,
        scratch_shapes=[pltpu.VMEM((8, 2048), BF), pltpu.SemaphoreType.DMA((CHIPS,))],
        compiler_params=LIMIT,
        name="combine",
    )(x, po, pll)


def project_kernel(a_ref, w_ref, x_ref, own_ref, other_ref):
    acc = jnp.zeros((256, 256), F32)
    top = (iota((256, 256), 0) & 7) < STEPS
    for half in range(2):
        part = jnp.zeros((256, 256), F32)
        for i in range(8):
            rows = pl.ds(half * 2048 + i * 256, 256)
            w = jnp.concatenate([w_ref[rows, :], x_ref[rows, :]], axis=1)
            part += mm(a_ref[:, pl.ds(i * 256, 256)], w)
        acc = jnp.where(top, part, acc) if half == 0 else jnp.where(top, acc, part)
    sub = iota((8, 256), 0)
    for k in range(16):
        a, b = acc[k * 16 : k * 16 + 8], acc[k * 16 + 8 : k * 16 + 16]
        a, b = a + pltpu.roll(a, STEPS, 0), b + pltpu.roll(b, STEPS, 0)
        both = jnp.where(sub < STEPS, a, b)
        own_ref[pl.ds(k * 8, 8), :] = both[:, :128]
        other_ref[pl.ds(k * 8, 8), :] = both[:, 128:]


def project(a, w, x):
    return pl.pallas_call(
        project_kernel,
        out_shape=[jax.ShapeDtypeStruct((128, 128), F32)] * 2,
        in_specs=[VM] * 3,
        out_specs=[VM] * 2,
        compiler_params=LIMIT,
        cost_estimate=pl.CostEstimate(
            flops=540_000_000, transcendentals=0, bytes_accessed=3_000_000
        ),
        name="project",
    )(a, w, x)


def order_kernel(own_ref, other_ref, out_ref):
    first = (lax.axis_index("req") & 1) == 0
    mine, theirs = own_ref[...], other_ref[...]
    even = jnp.where(first, mine, theirs)
    odd = jnp.where(first, theirs, mine)
    sub = iota((8, 128), 0)
    for k in range(16):
        a, b = even[k * 8 : k * 8 + 8], odd[k * 8 : k * 8 + 8]
        out_ref[pl.ds(k * 16, 8), :] = jnp.where(sub < STEPS, a, pltpu.roll(b, STEPS, 0))
        out_ref[pl.ds(k * 16 + 8, 8), :] = jnp.where(sub < STEPS, pltpu.roll(a, STEPS, 0), b)


def in_order(own, other):
    return pl.pallas_call(
        order_kernel,
        out_shape=jax.ShapeDtypeStruct((REQS * STEPS, 128), F32),
        in_specs=[VM] * 2,
        out_specs=VM,
        compiler_params=LIMIT,
        name="in_order",
    )(own, other)


def over_chips(x):
    return lax.all_to_all(
        x, "req", split_axis=0, concat_axis=0, axis_index_groups=SAME_CORE, tiled=True
    )


def swap_cores(x):
    return lax.ppermute(x, "req", CORE_SWAP)


def local(queries, nk, nv, pk, pv, hk, hv, kept, membership, out_weight):
    packed, own = pack(membership, queries)
    pk1, pv1, w1 = swap_cores(pk), swap_cores(pv), swap_cores(out_weight)
    q = over_chips(packed)
    po, pll = private(own, kept, hk, hv, nk, nv)
    q, po, pll = lax.optimization_barrier((q, po, pll))
    parts = over_chips(prefix(q, pk, pv, pk1, pv1))
    att = over_chips(combine(parts, po, pll))
    mine, other = project(att.reshape(256, 2048), out_weight, w1)
    part = in_order(mine, swap_cores(other))
    theirs = lax.ppermute(part, "kvh", [(0, 1), (1, 0)])
    return (part + theirs).astype(BF).reshape(REQS, STEPS, 128)


def solution(mesh):
    placed = (
        P("req", None, "kvh"),
        P("req", None, "kvh"),
        P("req", None, "kvh"),
        P(None, "req", "kvh"),
        P(None, "req", "kvh"),
        P("req", None, "kvh"),
        P("req", None, "kvh"),
        P("req", "kvh", None),
        P("req", None),
        P("kvh", "req"),
    )
    return jax.shard_map(
        local, mesh=mesh, in_specs=placed, out_specs=P(None, None, "req"), check_vma=False
    )
```

time: 132 us -> 94.1 us (0.71); the launches traced: 130 us -> 94 us
  blocking collectives: 68.9 us -> 0 us
  waiting for transfers between devices: 3.13 us -> 44.5 us
  Pallas kernels: 43.2 us -> 17.7 us
  starting transfers between devices: 8.54 us -> 28 us
  local copies, waits for them, and re-layouts: 4.35 us -> 2.36 us
    all_to_all x3 -> x0, blocking collectives: 68.9 us -> none  [over_chips(): lax.all_to_all(x, 'req', split_axis=0, concat_axis=0, axis_index_groups=S...]
    all_to_all x0 -> x3, waiting for transfers between devices: none -> 40.1 us  [over_chips(): lax.all_to_all(x, 'req', split_axis=0, concat_axis=0, axis_index_groups=S...]
    pallas_call x7 -> x5, Pallas kernels: 37.5 us -> 15 us  [the longest x1 10.7 us: prefix(): pl.pallas_call(prefix_kernel, out_shape=jax.ShapeDtypeStruct((CHIPS, PAY,...]
    all_to_all x0 -> x3, starting transfers between devices: none -> 18 us  [over_chips(): lax.all_to_all(x, 'req', split_axis=0, concat_axis=0, axis_index_groups=S...]
    pallas_call x1, Pallas kernels: 5.66 us -> 2.75 us  [private(): pl.pallas_call(private_kernel, out_shape=[jax.ShapeDtypeStruct((4, ROWS,...]
    ppermute x4, starting transfers between devices: 5.16 us -> 6.63 us  [swap_cores(): return lax.ppermute(x, 'req', CORE_SWAP)]
    slice x1 -> x0, local copies, waits for them, and re-layouts: 1.37 us -> none  [private(): packed[:1]]
    unnamed x12 -> x14, local copies, waits for them, and re-layouts: 2.98 us -> 2.36 us
  transfers between devices with their start and end apart: 5 -> 8, of which waited for: 1 -> 5; matrix products, arithmetic and copies ran while one was open for 1% -> 0% of each run, Pallas kernels for 16% -> 7%
where the time goes in v3:
time: 94.1 us; the launch traced here: 94 us
  waiting for transfers between devices  44.5 us (47%)
  starting transfers between devices  28 us (30%)
  Pallas kernels  17.7 us (19%)
  local copies, waits for them, and re-layouts  2.36 us (3%)
    all_to_all x3, waiting for transfers between devices, over_chips(): lax.all_to_all(x, 'req', split_axis=0, concat_axis=0, axis_index_groups=S...  40.1 us
    all_to_all x3, starting transfers between devices, over_chips(): lax.all_to_all(x, 'req', split_axis=0, concat_axis=0, axis_index_groups=S...  18 us
    pallas_call x1, Pallas kernels, prefix(): pl.pallas_call(prefix_kernel, out_shape=jax.ShapeDtypeStruct((CHIPS, PAY,...  10.7 us
    ppermute x4, starting transfers between devices, swap_cores(): return lax.ppermute(x, 'req', CORE_SWAP)  6.63 us
    ppermute x1, waiting for transfers between devices, local(): theirs = lax.ppermute(part, 'kvh', [(0, 1), (1, 0)])  3.52 us
    ppermute x1, starting transfers between devices, local(): theirs = lax.ppermute(part, 'kvh', [(0, 1), (1, 0)])  3.39 us
    pallas_call x1, Pallas kernels, private(): pl.pallas_call(private_kernel, out_shape=[jax.ShapeDtypeStruct((4, ROWS,...  2.75 us
    unnamed x14, local copies, waits for them, and re-layouts  2.36 us
  transfers between devices with their start and end apart: 8, of which 5 were waited for; matrix products, arithmetic and copies ran while one was open for 0% of the time, Pallas kernels for 7%

profile of v3, /device:TPU:1, one launch (start us, length us, event | category | flops | bytes accessed | tf_op | source)
XLA Modules:
  0.0 94.0 jit_solution(1069550828094253666)
XLA Ops:
  0.0 1.4 %collective-permute-start = (bf16[8,256,512]{2,1,0:T(8,128)(2,1)}, bf16[8,256,512]{2,1,0:T(8,128)(2,1)}, u32[]{:S(2)}, u32[]{:S(2)}) collective-permute-start(bf16[8,256,512]{2,1,0:T(8,128)(2,1)} %k0h.1), channel_id=1, source_target_pairs={{0,2},{2,0},{4,6},{6,4},{8,10},{10,8},{12,14},{14,12},{16,18},{18,... | collective-permute-start | bytes 6291464 | tf_op jit(solution)/shard_map/ppermute | solution.py:340
  1.4 0.0 collective-permute-start.1
  2.0 0.0 copy-start.3
  2.0 0.7 copy-done.3
  2.8 1.3 %pack.1 = (bf16[32,136,128]{2,1,0:T(8,128)(2,1)}, bf16[128,128]{1,0:T(8,128)(2,1)S(1)}) custom-call(s32[1,1]{1,0:T(1,128)S(6)} %copy.11.mem_ref, bf16[1,4,4096]{2,1,0:T(4,128)(2,1)S(1)} %copy-done.3), custom_call_target="tpu_custom_call" | custom-call | tf_op jit(solution)/shard_map/pack/pallas_call | solution.py:71
  4.1 8.6 %all-to-all-start = ((bf16[32,136,128]{2,1,0:T(8,128)(2,1)}), bf16[32,136,128]{2,1,0:T(8,128)(2,1)S(1)}, u32[]{:S(2)}, u32[]{:S(2)}) async-start(bf16[32,136,128]{2,1,0:T(8,128)(2,1)} %get-tuple-element.14), calls=%async_computation | async-start | bytes 2228224 | tf_op jit(solution)/shard_map/all_to_all | solution.py:334
  12.7 0.0 copy-done
  12.7 0.0 copy-done.4
  12.8 0.0 copy-done.5
  12.8 0.0 copy-done.6
  12.8 0.0 copy-start.1
  12.8 1.6 %copy-done.1 = bf16[1,2048,512]{2,1,0:T(8,128)(2,1)S(1)} copy-done((bf16[1,2048,512]{2,1,0:T(8,128)(2,1)S(1)}, bf16[1,2048,512]{2,1,0:T(8,128)(2,1)}, u32[]{:S(2)}) %copy-start.1) | copy-done | bytes 2097176
  14.4 2.7 %private.1 = (f32[4,32,128]{2,1,0:T(8,128)S(1)}, f32[4,32,128]{2,1,0:T(8,128)S(1)}) custom-call(bf16[128,128]{1,0:T(8,128)(2,1)S(1)} %get-tuple-element.15.q_ref, s32[1,4,1024]{2,1,0:T(4,128)S(1)} %copy-done.4, bf16[1,2048,512]{2,1,0:T(8,128)(2,1)S(1)} %copy-done, bf16[1,2048,512]{2,1,0:T(8,128)(2,1)S(1)} %copy-done.1, bf16[1,4,512]{2,1,0:T(4,128)(2,1)S(1)} %copy-done.5, ...), custom_call_target="tpu_custom_call" | custom-call | flops 400000000 | bytes 5000000 | tf_op jit(solution)/shard_map/private/pallas_call | solution.py:128
  17.1 11.7 %all-to-all-done.q = bf16[32,136,128]{2,1,0:T(8,128)(2,1)S(1)} async-done(((bf16[32,136,128]{2,1,0:T(8,128)(2,1)}), bf16[32,136,128]{2,1,0:T(8,128)(2,1)S(1)}, u32[]{:S(2)}, u32[]{:S(2)}) %all-to-all-start) | async-done | bytes 1114144 | tf_op jit(solution)/shard_map/all_to_all | solution.py:334
  28.8 0.0 collective-permute-done.k1h
  28.8 0.0 collective-permute-done.1.v1h
  28.8 10.7 %prefix.1 = bf16[32,136,128]{2,1,0:T(8,128)(2,1)} custom-call(bf16[32,136,128]{2,1,0:T(8,128)(2,1)S(1)} %all-to-all-done.q, bf16[8,256,512]{2,1,0:T(8,128)(2,1)} %k0h.1, bf16[8,256,512]{2,1,0:T(8,128)(2,1)} %v0h.1, bf16[8,256,512]{2,1,0:T(8,128)(2,1)} %collective-permute-done.k1h, bf16[8,256,512]{2,1,0:T(8,128)(2,1)} %collective-permute-done.1.v1h), custom_call_target="tpu_custom_call" | custom-call | flops 1200000000 | bytes 10000000 | tf_op jit(solution)/shard_map/prefix/pallas_call | solution.py:218
  39.5 0.0 copy-start.2
  39.5 4.9 %all-to-all-start.1 = ((bf16[32,136,128]{2,1,0:T(8,128)(2,1)}), bf16[32,136,128]{2,1,0:T(8,128)(2,1)S(1)}, u32[]{:S(2)}, u32[]{:S(2)}) async-start(bf16[32,136,128]{2,1,0:T(8,128)(2,1)} %prefix.1), calls=%async_computation.1 | async-start | bytes 2228224 | tf_op jit(solution)/shard_map/all_to_all | solution.py:334
  44.4 0.0 copy-done.2
  44.4 1.3 %collective-permute-start.2 = (bf16[4096,128]{1,0:T(8,128)(2,1)S(1)}, bf16[4096,128]{1,0:T(8,128)(2,1)S(1)}, u32[]{:S(2)}, u32[]{:S(2)}) collective-permute-start(bf16[4096,128]{1,0:T(8,128)(2,1)S(1)} %copy-done.2), channel_id=1, source_target_pairs={{0,2},{2,0},{4,6},{6,4},{8,10},{10,8},{12,14},{14,12},{16,18},{18,... | collective-permute-start | bytes 3145736 | tf_op jit(solution)/shard_map/ppermute | solution.py:340
  45.7 14.6 %all-to-all-done.1.in_ref = bf16[32,136,128]{2,1,0:T(8,128)(2,1)S(1)} async-done(((bf16[32,136,128]{2,1,0:T(8,128)(2,1)}), bf16[32,136,128]{2,1,0:T(8,128)(2,1)S(1)}, u32[]{:S(2)}, u32[]{:S(2)}) %all-to-all-start.1) | async-done | bytes 1114144 | tf_op jit(solution)/shard_map/all_to_all | solution.py:334
  60.3 2.2 %combine.1 = bf16[32,8,2048]{2,1,0:T(8,128)(2,1)} custom-call(bf16[32,136,128]{2,1,0:T(8,128)(2,1)S(1)} %all-to-all-done.1.in_ref, f32[4,32,128]{2,1,0:T(8,128)S(1)} %get-tuple-element.19.po_ref, f32[4,32,128]{2,1,0:T(8,128)S(1)} %get-tuple-element.20.pl_ref), custom_call_target="tpu_custom_call" | custom-call | tf_op jit(solution)/shard_map/combine/pallas_call | solution.py:266
  62.5 4.5 %all-to-all-start.2 = ((bf16[32,8,2048]{2,1,0:T(8,128)(2,1)}), bf16[32,8,2048]{2,1,0:T(8,128)(2,1)S(1)}, u32[]{:S(2)}, u32[]{:S(2)}) async-start(bf16[32,8,2048]{2,1,0:T(8,128)(2,1)} %combine.1), calls=%async_computation.2 | async-start | bytes 2097152 | tf_op jit(solution)/shard_map/all_to_all | solution.py:334
  67.0 0.0 collective-permute-done.2.x_ref
  67.0 13.8 %all-to-all-done.2 = bf16[32,8,2048]{2,1,0:T(8,128)(2,1)S(1)} async-done(((bf16[32,8,2048]{2,1,0:T(8,128)(2,1)}), bf16[32,8,2048]{2,1,0:T(8,128)(2,1)S(1)}, u32[]{:S(2)}, u32[]{:S(2)}) %all-to-all-start.2) | async-done | bytes 1048608 | tf_op jit(solution)/shard_map/all_to_all | solution.py:334
  80.8 0.7 project.1
  81.5 4.0 %collective-permute-start.3 = (f32[128,128]{1,0:T(8,128)S(1)}, f32[128,128]{1,0:T(8,128)S(1)}, u32[]{:S(2)}, u32[]{:S(2)}) collective-permute-start(f32[128,128]{1,0:T(8,128)S(1)} %get-tuple-element.22), channel_id=1, source_target_pairs={{0,2},{2,0},{4,6},{6,4},{8,10},{10,8},{12,14},{14,12},{16,18},{18,... | collective-permute-start | bytes 196616 | tf_op jit(solution)/shard_map/ppermute | solution.py:340
  85.5 0.9 collective-permute-done.3.other_ref
  86.4 3.4 %collective-permute-start.4 = (f32[256,128]{1,0:T(8,128)S(1)}, f32[256,128]{1,0:T(8,128)S(1)}, u32[]{:S(2)}, u32[]{:S(2)}) collective-permute-start(f32[256,128]{1,0:T(8,128)S(1)} %in_order.1), channel_id=1, source_target_pairs={{0,1},{1,0},{2,3},{3,2},{4,5},{5,4},{6,7},{7,6},{8,9},{9,8},{10,11... | collective-permute-start | bytes 393224 | tf_op jit(solution)/shard_map/ppermute | solution.py:353
  89.8 3.5 %collective-permute-done.4 = f32[256,128]{1,0:T(8,128)S(1)} collective-permute-done((f32[256,128]{1,0:T(8,128)S(1)}, f32[256,128]{1,0:T(8,128)S(1)}, u32[]{:S(2)}, u32[]{:S(2)}) %collective-permute-start.4) | collective-permute-done | bytes 131104 | tf_op jit(solution)/shard_map/ppermute | solution.py:353
  93.3 0.7 add_convert_fusion
  (5 shorter events, 0.0 us)
Async XLA Ops:
  0.0 12.7 %copy-start = (bf16[1,2048,512]{2,1,0:T(8,128)(2,1)S(1)}, bf16[1,2048,512]{2,1,0:T(8,128)(2,1)}, u32[]{:S(2)}) copy-start(bf16[1,2048,512]{2,1,0:T(8,128)(2,1)} %hk_ref.1) | copy-start | bytes 6291460
  0.0 28.8 %collective-permute-start = (bf16[8,256,512]{2,1,0:T(8,128)(2,1)}, bf16[8,256,512]{2,1,0:T(8,128)(2,1)}, u32[]{:S(2)}, u32[]{:S(2)}) collective-permute-start(bf16[8,256,512]{2,1,0:T(8,128)(2,1)} %k0h.1), channel_id=1, source_target_pairs={{0,2},{2,0},{4,6},{6,4},{8,10},{10,8},{12,14},{14,12},{16,18},{18,... | collective-permute-start | bytes 6291464 | tf_op jit(solution)/shard_map/ppermute | solution.py:340
  1.4 27.4 %collective-permute-start.1 = (bf16[8,256,512]{2,1,0:T(8,128)(2,1)}, bf16[8,256,512]{2,1,0:T(8,128)(2,1)}, u32[]{:S(2)}, u32[]{:S(2)}) collective-permute-start(bf16[8,256,512]{2,1,0:T(8,128)(2,1)} %v0h.1), channel_id=1, source_target_pairs={{0,2},{2,0},{4,6},{6,4},{8,10},{10,8},{12,14},{14,12},{16,18},{18,... | collective-permute-start | bytes 6291464 | tf_op jit(solution)/shard_map/ppermute | solution.py:340
  2.0 0.8 copy-start.3
  2.8 10.0 %copy-start.4 = (s32[1,4,1024]{2,1,0:T(4,128)S(1)}, s32[1,4,1024]{2,1,0:T(4,128)}, u32[]{:S(2)}) copy-start(s32[1,4,1024]{2,1,0:T(4,128)} %kept_ref.1) | copy-start | bytes 49156
  2.8 10.0 %copy-start.5 = (bf16[1,4,512]{2,1,0:T(4,128)(2,1)S(1)}, bf16[1,4,512]{2,1,0:T(4,128)(2,1)}, u32[]{:S(2)}) copy-start(bf16[1,4,512]{2,1,0:T(4,128)(2,1)} %nk_ref.1) | copy-start | bytes 12292
  2.8 10.0 %copy-start.6 = (bf16[1,4,512]{2,1,0:T(4,128)(2,1)S(1)}, bf16[1,4,512]{2,1,0:T(4,128)(2,1)}, u32[]{:S(2)}) copy-start(bf16[1,4,512]{2,1,0:T(4,128)(2,1)} %nv_ref.1) | copy-start | bytes 12292
  4.1 24.7 %all-to-all-start = ((bf16[32,136,128]{2,1,0:T(8,128)(2,1)}), bf16[32,136,128]{2,1,0:T(8,128)(2,1)S(1)}, u32[]{:S(2)}, u32[]{:S(2)}) async-start(bf16[32,136,128]{2,1,0:T(8,128)(2,1)} %get-tuple-element.14), calls=%async_computation | async-start | bytes 2228224 | tf_op jit(solution)/shard_map/all_to_all | solution.py:334
  12.8 1.6 %copy-start.1 = (bf16[1,2048,512]{2,1,0:T(8,128)(2,1)S(1)}, bf16[1,2048,512]{2,1,0:T(8,128)(2,1)}, u32[]{:S(2)}) copy-start(bf16[1,2048,512]{2,1,0:T(8,128)(2,1)} %hv_ref.1) | copy-start | bytes 6291460
  39.5 4.9 %copy-start.2 = (bf16[4096,128]{1,0:T(8,128)(2,1)S(1)}, bf16[4096,128]{1,0:T(8,128)(2,1)}, u32[]{:S(2)}) copy-start(bf16[4096,128]{1,0:T(8,128)(2,1)} %w_ref.1) | copy-start | bytes 3145732
  39.5 20.7 %all-to-all-start.1 = ((bf16[32,136,128]{2,1,0:T(8,128)(2,1)}), bf16[32,136,128]{2,1,0:T(8,128)(2,1)S(1)}, u32[]{:S(2)}, u32[]{:S(2)}) async-start(bf16[32,136,128]{2,1,0:T(8,128)(2,1)} %prefix.1), calls=%async_computation.1 | async-start | bytes 2228224 | tf_op jit(solution)/shard_map/all_to_all | solution.py:334
  44.4 22.6 %collective-permute-start.2 = (bf16[4096,128]{1,0:T(8,128)(2,1)S(1)}, bf16[4096,128]{1,0:T(8,128)(2,1)S(1)}, u32[]{:S(2)}, u32[]{:S(2)}) collective-permute-start(bf16[4096,128]{1,0:T(8,128)(2,1)S(1)} %copy-done.2), channel_id=1, source_target_pairs={{0,2},{2,0},{4,6},{6,4},{8,10},{10,8},{12,14},{14,12},{16,18},{18,... | collective-permute-start | bytes 3145736 | tf_op jit(solution)/shard_map/ppermute | solution.py:340
  62.5 18.3 %all-to-all-start.2 = ((bf16[32,8,2048]{2,1,0:T(8,128)(2,1)}), bf16[32,8,2048]{2,1,0:T(8,128)(2,1)S(1)}, u32[]{:S(2)}, u32[]{:S(2)}) async-start(bf16[32,8,2048]{2,1,0:T(8,128)(2,1)} %combine.1), calls=%async_computation.2 | async-start | bytes 2097152 | tf_op jit(solution)/shard_map/all_to_all | solution.py:334
  81.5 4.9 %collective-permute-start.3 = (f32[128,128]{1,0:T(8,128)S(1)}, f32[128,128]{1,0:T(8,128)S(1)}, u32[]{:S(2)}, u32[]{:S(2)}) collective-permute-start(f32[128,128]{1,0:T(8,128)S(1)} %get-tuple-element.22), channel_id=1, source_target_pairs={{0,2},{2,0},{4,6},{6,4},{8,10},{10,8},{12,14},{14,12},{16,18},{18,... | collective-permute-start | bytes 196616 | tf_op jit(solution)/shard_map/ppermute | solution.py:340
  86.4 6.9 %collective-permute-start.4 = (f32[256,128]{1,0:T(8,128)S(1)}, f32[256,128]{1,0:T(8,128)S(1)}, u32[]{:S(2)}, u32[]{:S(2)}) collective-permute-start(f32[256,128]{1,0:T(8,128)S(1)} %in_order.1), channel_id=1, source_target_pairs={{0,1},{1,0},{2,3},{3,2},{4,5},{5,4},{6,7},{7,6},{8,9},{9,8},{10,11... | collective-permute-start | bytes 393224 | tf_op jit(solution)/shard_map/ppermute | solution.py:353

commit v4 on v3

--- a/solution.py
+++ b/solution.py
@@ -15,6 +15,7 @@
 HISTORY = 2048
 KEPT = 1024
 GROUP = 4
+UNROLL = 2
 PAY = 136
 LOG2E = 1.4426950408889634
 C2 = HEAD ** -0.5 * LOG2E
@@ -28,7 +29,6 @@
 LIMIT = pltpu.CompilerParams(vmem_limit_bytes=24 << 20)
 
 VM = pl.BlockSpec(memory_space=pltpu.VMEM)
-SM = pl.BlockSpec(memory_space=pltpu.SMEM)
 HB = pl.BlockSpec(memory_space=pltpu.HBM)
 
 
@@ -56,7 +56,10 @@
         copy.wait()
 
 
-def pack_kernel(mem_ref, q_ref, out_ref, own_ref, tmp, tile, sem):
+def pack_kernel(mem_ref, q_hbm, out_ref, own_ref, q_ref, tmp, tile, sem, in_sem):
+    cq = pltpu.make_async_copy(q_hbm, q_ref, in_sem)
+    cq.start()
+    cq.wait()
     for head in range(32):
         tmp[pl.ds(head * STEPS, STEPS), :] = q_ref[0, :, pl.ds(head * HEAD, HEAD)].astype(F32)
     data = tmp[...].astype(BF)
@@ -74,16 +77,18 @@
             pltpu.HBM((CHIPS, PAY, HEAD), BF),
             jax.ShapeDtypeStruct((128, HEAD), BF),
         ],
-        in_specs=[SM, VM],
+        in_specs=[pl.BlockSpec(memory_space=pltpu.SMEM), HB],
         out_specs=[HB, VM],
         scratch_shapes=[
+            pltpu.VMEM((1, STEPS, 32 * HEAD), BF),
             pltpu.VMEM((128, HEAD), F32),
             pltpu.VMEM((PAY, HEAD), BF),
             pltpu.SemaphoreType.DMA((CHIPS,)),
+            pltpu.SemaphoreType.DMA(()),
         ],
         compiler_params=LIMIT,
         name="pack",
-    )(membership, queries)
+    )(membership, in_hbm(queries))
 
 
 def private_kernel(q_ref, kept_ref, hk_ref, hv_ref, nk_ref, nv_ref, o_ref, l_ref, knew, vnew):
@@ -162,46 +167,58 @@
         return jnp.sum(x, axis=0, keepdims=True)
 
     order = total(jnp.where(here, row.astype(F32), 0.0))
-    starts = total(jnp.where(member < lanef, 1.0, 0.0))
     counts = total(jnp.where(member == lanef, 1.0, 0.0))
-    table = jnp.concatenate([order, starts, counts, jnp.zeros((5, 128), F32)], axis=0)
+    p8, l8 = iota((8, 128), 0).astype(F32), lanef[:8]
+    parts = jnp.where(l8 < PROMPTS, jnp.floor((counts + (GROUP - 1.0)) * (1.0 / GROUP)), 0.0)
+
+    def along(x):
+        return jnp.sum(x, axis=1, keepdims=True)
+
+    until = along(jnp.where(l8 <= p8, parts, 0.0))
+    since = until - along(jnp.where(l8 == p8, parts, 0.0))
+    starts = along(jnp.where(across[:8] < p8, 1.0, 0.0))
+    groups = total(jnp.where(p8 == PROMPTS - 1.0, until, 0.0))
+    at = jnp.minimum(l8, groups - 1.0)
+    inside = (at >= since) & (at < until)
+    prompts = total(jnp.where(inside, p8, 0.0))
+    firsts = total(jnp.where(inside, starts + GROUP * (at - since), 0.0))
+    table = jnp.concatenate([order, prompts, firsts, groups, jnp.zeros((4, 128), F32)], axis=0)
     tab_v[...] = table.astype(jnp.int32)
     ct = pltpu.make_async_copy(tab_v, tab_s, tsem)
     ct.start()
     ct.wait()
 
-    ones = jnp.ones((PORTION, HEAD), BF)
-
-    def prompt(p, carry):
+    ones = jnp.ones((2 * PORTION, HEAD), BF)
+
+    def arrive(p, c):
         for copy in fetch(p):
             copy.wait()
-        start = tab_s[1, p]
-        chunks = (tab_s[2, p] + GROUP - 1) // GROUP
-
-        def chunk(i, c):
-            slot0 = start + i * GROUP
+        return c
+
+    def several(i, seen):
+        ps = [tab_s[1, i * UNROLL + u] for u in range(UNROLL)]
+        lax.fori_loop(seen, ps[-1] + 1, arrive, 0)
+        for u in range(UNROLL):
+            p, slot0 = ps[u], tab_s[2, i * UNROLL + u]
             at = [tab_s[0, slot0 + j] for j in range(GROUP)]
             for g in range(4):
                 rows, lanes = pl.ds(g * ROWS, ROWS), pl.ds(g * HEAD, HEAD)
                 qs = jnp.concatenate([q[t, rows, :] for t in at], axis=0)
-                s0 = nt(qs, k0[p, :, lanes])
-                s1 = nt(qs, k1[p, :, lanes])
-                peak = jnp.maximum(jnp.max(s0, axis=1, keepdims=True), jnp.max(s1, axis=1, keepdims=True))
-                w0 = jnp.exp2((s0 - peak) * C2).astype(BF)
-                w1 = jnp.exp2((s1 - peak) * C2).astype(BF)
-                ov = mm(w0, jnp.concatenate([v0[p, :, lanes], ones], axis=1))
-                ov += mm(w1, jnp.concatenate([v1[p, :, lanes], ones], axis=1))
+                s = jnp.concatenate([nt(qs, k0[p, :, lanes]), nt(qs, k1[p, :, lanes])], axis=1)
+                peak = jnp.max(s, axis=1, keepdims=True)
+                w = jnp.exp2((s - peak) * C2).astype(BF)
+                v = jnp.concatenate([v0[p, :, lanes], v1[p, :, lanes]], axis=0)
+                ov = mm(w, jnp.concatenate([v, ones], axis=1))
                 l = ov[:, HEAD:]
                 o = (ov[:, :HEAD] / l).astype(BF)
                 lse = peak * C2 + jnp.log(l) * LOG2E
                 for j in reversed(range(GROUP)):
                     out_ref[at[j], rows, :] = o[j * ROWS : (j + 1) * ROWS]
                     lbuf[at[j], rows, :] = lse[j * ROWS : (j + 1) * ROWS]
-            return c
-
-        return lax.fori_loop(0, chunks, chunk, carry)
-
-    lax.fori_loop(0, PROMPTS, prompt, 0)
+        return ps[-1] + 1
+
+    seen = lax.fori_loop(0, (tab_s[3, 0] + UNROLL - 1) // UNROLL, several, 0)
+    lax.fori_loop(seen, PROMPTS, arrive, 0)
 
     diag = row == lane
     sub = iota((8, 128), 0)
@@ -236,7 +253,7 @@
     )(q, in_hbm(k0), in_hbm(v0), k1, v1)
 
 
-def combine_kernel(in_ref, po_ref, pl_ref, out_ref, tile, sem):
+def combine_kernel(in_ref, po_ref, pl_ref, out_ref):
     row, lane = iota((128, 128), 0), iota((128, 128), 1)
     own = jnp.sum(jnp.where(row == lane, pl_ref[...].reshape(128, 128), 0.0), axis=0, keepdims=True)
     pieces = [in_ref[n, pl.ds(128, 8), :].astype(F32) for n in range(CHIPS)]
@@ -258,8 +275,9 @@
             tiles.append(jnp.where(sub < STEPS, a, pltpu.roll(b, STEPS, 0)))
         else:
             tiles.append(jnp.where(sub < STEPS, pltpu.roll(a, STEPS, 0), b))
-    tile[...] = jnp.concatenate(tiles, axis=1).astype(BF)
-    spread(tile, out_ref, sem)
+    att = jnp.concatenate(tiles, axis=1).astype(BF)
+    for n in range(CHIPS):
+        out_ref[n] = att
 
 
 def combine(x, po, pll):
@@ -267,8 +285,7 @@
         combine_kernel,
         out_shape=jax.ShapeDtypeStruct((CHIPS, 8, 2048), BF),
         in_specs=[VM] * 3,
-        out_specs=HB,
-        scratch_shapes=[pltpu.VMEM((8, 2048), BF), pltpu.SemaphoreType.DMA((CHIPS,))],
+        out_specs=VM,
         compiler_params=LIMIT,
         name="combine",
     )(x, po, pll)
@@ -345,7 +362,7 @@
     pk1, pv1, w1 = swap_cores(pk), swap_cores(pv), swap_cores(out_weight)
     q = over_chips(packed)
     po, pll = private(own, kept, hk, hv, nk, nv)
-    q, po, pll = lax.optimization_barrier((q, po, pll))
+    q, po, pll, w1 = lax.optimization_barrier((q, po, pll, w1))
     parts = over_chips(prefix(q, pk, pv, pk1, pv1))
     att = over_chips(combine(parts, po, pll))
     mine, other = project(att.reshape(256, 2048), out_weight, w1)

time: 94.1 us -> 91 us (0.967)
  blocking collectives: 0 us -> 40.7 us
  waiting for transfers between devices: 44.5 us -> 14.4 us
  starting transfers between devices: 28 us -> 17.2 us
  Pallas kernels: 17.7 us -> 14.3 us
    all_to_all x0 -> x2, blocking collectives: none -> 40.7 us  [over_chips(): lax.all_to_all(x, 'req', split_axis=0, concat_axis=0, axis_index_groups=S...]
    all_to_all x3 -> x1, waiting for transfers between devices: 40.1 us -> 10 us  [over_chips(): lax.all_to_all(x, 'req', split_axis=0, concat_axis=0, axis_index_groups=S...]
    all_to_all x3 -> x1, starting transfers between devices: 18 us -> 8.53 us  [over_chips(): lax.all_to_all(x, 'req', split_axis=0, concat_axis=0, axis_index_groups=S...]
    pallas_call x1, Pallas kernels: 10.7 us -> 7.76 us  [prefix(): pl.pallas_call(prefix_kernel, out_shape=jax.ShapeDtypeStruct((CHIPS, PAY,...]
    ppermute x4, starting transfers between devices: 6.63 us -> 5.31 us  [swap_cores(): return lax.ppermute(x, 'req', CORE_SWAP)]
    pallas_call x1, Pallas kernels: 2.22 us -> 1.03 us  [combine(): pl.pallas_call(combine_kernel, out_shape=jax.ShapeDtypeStruct((CHIPS, 8,...]
    unnamed x14 -> x16, local copies, waits for them, and re-layouts: 2.36 us -> 2.59 us
  transfers between devices with their start and end apart: 8 -> 6, of which waited for: 5 -> 3; matrix products, arithmetic and copies ran while one was open for 0% -> 0% of each run, Pallas kernels for 7% -> 5%
where the time goes in v4:
time: 91 us; the launch traced here: 90.7 us
  blocking collectives  40.7 us (45%)
  starting transfers between devices  17.2 us (19%)
  waiting for transfers between devices  14.4 us (16%)
  Pallas kernels  14.3 us (16%)
  local copies, waits for them, and re-layouts  2.59 us (3%)
    all_to_all x2, blocking collectives, over_chips(): lax.all_to_all(x, 'req', split_axis=0, concat_axis=0, axis_index_groups=S...  40.7 us
    all_to_all x1, waiting for transfers between devices, over_chips(): lax.all_to_all(x, 'req', split_axis=0, concat_axis=0, axis_index_groups=S...  10 us
    all_to_all x1, starting transfers between devices, over_chips(): lax.all_to_all(x, 'req', split_axis=0, concat_axis=0, axis_index_groups=S...  8.53 us
    pallas_call x1, Pallas kernels, prefix(): pl.pallas_call(prefix_kernel, out_shape=jax.ShapeDtypeStruct((CHIPS, PAY,...  7.76 us
    ppermute x4, starting transfers between devices, swap_cores(): return lax.ppermute(x, 'req', CORE_SWAP)  5.31 us
    ppermute x1, waiting for transfers between devices, local(): theirs = lax.ppermute(part, 'kvh', [(0, 1), (1, 0)])  3.52 us
    ppermute x1, starting transfers between devices, local(): theirs = lax.ppermute(part, 'kvh', [(0, 1), (1, 0)])  3.38 us
    pallas_call x1, Pallas kernels, private(): pl.pallas_call(private_kernel, out_shape=[jax.ShapeDtypeStruct((4, ROWS,...  2.75 us
  transfers between devices with their start and end apart: 6, of which 3 were waited for; matrix products, arithmetic and copies ran while one was open for 0% of the time, Pallas kernels for 5%

profile of v4, /device:TPU:1, one launch (start us, length us, event | category | flops | bytes accessed | tf_op | source)
XLA Modules:
  0.0 90.7 jit_solution(2605935410058640211)
XLA Ops:
  0.0 0.0 copy-start.5
  0.0 0.0 copy-start.6
  0.0 1.4 %collective-permute-start.1 = (bf16[8,256,512]{2,1,0:T(8,128)(2,1)}, bf16[8,256,512]{2,1,0:T(8,128)(2,1)}, u32[]{:S(2)}, u32[]{:S(2)}) collective-permute-start(bf16[8,256,512]{2,1,0:T(8,128)(2,1)} %k0h.1), channel_id=1, source_target_pairs={{0,2},{2,0},{4,6},{6,4},{8,10},{10,8},{12,14},{14,12},{16,18},{18,... | collective-permute-start | bytes 6291464 | tf_op jit(solution)/shard_map/ppermute | solution.py:357
  1.5 0.1 collective-permute-start.2
  2.2 2.1 %pack.1 = (bf16[32,136,128]{2,1,0:T(8,128)(2,1)}, bf16[128,128]{1,0:T(8,128)(2,1)S(1)}) custom-call(s32[1,1]{1,0:T(1,128)S(6)} %copy.11.mem_ref, bf16[1,4,4096]{2,1,0:T(4,128)(2,1)} %q_hbm.1), custom_call_target="tpu_custom_call" | custom-call | tf_op jit(solution)/shard_map/pack/pallas_call | solution.py:74
  4.3 8.5 %all-to-all-start = ((bf16[32,136,128]{2,1,0:T(8,128)(2,1)}), bf16[32,136,128]{2,1,0:T(8,128)(2,1)S(1)}, u32[]{:S(2)}, u32[]{:S(2)}) async-start(bf16[32,136,128]{2,1,0:T(8,128)(2,1)} %get-tuple-element.15), calls=%async_computation | async-start | bytes 2228224 | tf_op jit(solution)/shard_map/all_to_all | solution.py:351
  12.8 0.8 collective-permute-start
  13.7 0.0 copy-done.5
  13.7 0.0 copy-done
  13.7 0.0 copy-done.7
  13.7 0.0 copy-done.6
  13.7 0.0 copy-start.1
  13.7 1.6 %copy-done.1 = bf16[1,2048,512]{2,1,0:T(8,128)(2,1)S(1)} copy-done((bf16[1,2048,512]{2,1,0:T(8,128)(2,1)S(1)}, bf16[1,2048,512]{2,1,0:T(8,128)(2,1)}, u32[]{:S(2)}) %copy-start.1) | copy-done | bytes 2097176
  15.3 2.7 %private.1 = (f32[4,32,128]{2,1,0:T(8,128)S(1)}, f32[4,32,128]{2,1,0:T(8,128)S(1)}) custom-call(bf16[128,128]{1,0:T(8,128)(2,1)S(1)} %get-tuple-element.16.q_ref, s32[1,4,1024]{2,1,0:T(4,128)S(1)} %copy-done.5, bf16[1,2048,512]{2,1,0:T(8,128)(2,1)S(1)} %copy-done, bf16[1,2048,512]{2,1,0:T(8,128)(2,1)S(1)} %copy-done.1, bf16[1,4,512]{2,1,0:T(4,128)(2,1)S(1)} %copy-done.6, ...), custom_call_target="tpu_custom_call" | custom-call | flops 400000000 | bytes 5000000 | tf_op jit(solution)/shard_map/private/pallas_call | solution.py:133
  18.0 0.0 collective-permute-done.x_ref
  18.0 0.0 copy-start.3
  18.0 1.0 %copy-done.3 = bf16[4096,128]{1,0:T(8,128)(2,1)} copy-done((bf16[4096,128]{1,0:T(8,128)(2,1)}, bf16[4096,128]{1,0:T(8,128)(2,1)S(1)}, u32[]{:S(2)}) %copy-start.3) | copy-done | bytes 1048600
  19.0 10.0 %all-to-all-done.q = bf16[32,136,128]{2,1,0:T(8,128)(2,1)S(1)} async-done(((bf16[32,136,128]{2,1,0:T(8,128)(2,1)}), bf16[32,136,128]{2,1,0:T(8,128)(2,1)S(1)}, u32[]{:S(2)}, u32[]{:S(2)}) %all-to-all-start) | async-done | bytes 1114144 | tf_op jit(solution)/shard_map/all_to_all | solution.py:351
  29.0 0.0 collective-permute-done.1.k1h
  29.0 0.0 collective-permute-done.2.v1h
  29.0 7.8 %prefix.1 = bf16[32,136,128]{2,1,0:T(8,128)(2,1)S(1)} custom-call(bf16[32,136,128]{2,1,0:T(8,128)(2,1)S(1)} %all-to-all-done.q, bf16[8,256,512]{2,1,0:T(8,128)(2,1)} %k0h.1, bf16[8,256,512]{2,1,0:T(8,128)(2,1)} %v0h.1, bf16[8,256,512]{2,1,0:T(8,128)(2,1)} %collective-permute-done.1.k1h, bf16[8,256,512]{2,1,0:T(8,128)(2,1)} %collective-permute-done.2.v1h), custom_call_target="tpu_custom_call" | custom-call | flops 1200000000 | bytes 10000000 | tf_op jit(solution)/shard_map/prefix/pallas_call | solution.py:235
  36.8 21.0 %all_to_all.15.in_ref = bf16[32,136,128]{2,1,0:T(8,128)(2,1)S(1)} all-to-all(bf16[32,136,128]{2,1,0:T(8,128)(2,1)S(1)} %prefix.1), channel_id=1, replica_groups={{0,4,8,12,16,20,24,28,32,36,40,44,48,52,56,60,64,68,72,76,80,84,88,92,9..., dimensions={0} | all-to-all | bytes 2228224 | tf_op jit(solution)/shard_map/all_to_all | solution.py:351
  57.8 1.0 %combine.1 = bf16[32,8,2048]{2,1,0:T(8,128)(2,1)S(1)} custom-call(bf16[32,136,128]{2,1,0:T(8,128)(2,1)S(1)} %all_to_all.15.in_ref, f32[4,32,128]{2,1,0:T(8,128)S(1)} %get-tuple-element.20.po_ref, f32[4,32,128]{2,1,0:T(8,128)S(1)} %get-tuple-element.21.pl_ref), custom_call_target="tpu_custom_call" | custom-call | tf_op jit(solution)/shard_map/combine/pallas_call | solution.py:284
  58.8 19.7 %all_to_all.16 = bf16[32,8,2048]{2,1,0:T(8,128)(2,1)S(1)} all-to-all(bf16[32,8,2048]{2,1,0:T(8,128)(2,1)S(1)} %combine.1), channel_id=1, replica_groups={{0,4,8,12,16,20,24,28,32,36,40,44,48,52,56,60,64,68,72,76,80,84,88,92,9..., dimensions={0} | all-to-all | bytes 2097152 | tf_op jit(solution)/shard_map/all_to_all | solution.py:351
  78.5 0.0 copy-done.2
  78.5 0.0 copy-done.4
  78.5 0.7 project.1
  79.2 2.9 %collective-permute-start.3 = (f32[128,128]{1,0:T(8,128)S(1)}, f32[128,128]{1,0:T(8,128)S(1)}, u32[]{:S(2)}, u32[]{:S(2)}) collective-permute-start(f32[128,128]{1,0:T(8,128)S(1)} %get-tuple-element.24), channel_id=1, source_target_pairs={{0,2},{2,0},{4,6},{6,4},{8,10},{10,8},{12,14},{14,12},{16,18},{18,... | collective-permute-start | bytes 196616 | tf_op jit(solution)/shard_map/ppermute | solution.py:357
  82.2 0.9 collective-permute-done.3.other_ref
  83.1 3.4 %collective-permute-start.4 = (f32[256,128]{1,0:T(8,128)S(1)}, f32[256,128]{1,0:T(8,128)S(1)}, u32[]{:S(2)}, u32[]{:S(2)}) collective-permute-start(f32[256,128]{1,0:T(8,128)S(1)} %in_order.1), channel_id=1, source_target_pairs={{0,1},{1,0},{2,3},{3,2},{4,5},{5,4},{6,7},{7,6},{8,9},{9,8},{10,11... | collective-permute-start | bytes 393224 | tf_op jit(solution)/shard_map/ppermute | solution.py:370
  86.5 3.5 %collective-permute-done.4 = f32[256,128]{1,0:T(8,128)S(1)} collective-permute-done((f32[256,128]{1,0:T(8,128)S(1)}, f32[256,128]{1,0:T(8,128)S(1)}, u32[]{:S(2)}, u32[]{:S(2)}) %collective-permute-start.4) | collective-permute-done | bytes 131104 | tf_op jit(solution)/shard_map/ppermute | solution.py:370
  90.0 0.7 add_convert_fusion
  (5 shorter events, 0.0 us)
Async XLA Ops:
  0.0 13.7 %copy-start.5 = (s32[1,4,1024]{2,1,0:T(4,128)S(1)}, s32[1,4,1024]{2,1,0:T(4,128)}, u32[]{:S(2)}) copy-start(s32[1,4,1024]{2,1,0:T(4,128)} %kept_ref.1) | copy-start | bytes 49156
  0.0 13.7 %copy-start = (bf16[1,2048,512]{2,1,0:T(8,128)(2,1)S(1)}, bf16[1,2048,512]{2,1,0:T(8,128)(2,1)}, u32[]{:S(2)}) copy-start(bf16[1,2048,512]{2,1,0:T(8,128)(2,1)} %hk_ref.1) | copy-start | bytes 6291460
  0.0 13.7 %copy-start.7 = (bf16[1,4,512]{2,1,0:T(4,128)(2,1)S(1)}, bf16[1,4,512]{2,1,0:T(4,128)(2,1)}, u32[]{:S(2)}) copy-start(bf16[1,4,512]{2,1,0:T(4,128)(2,1)} %nv_ref.1) | copy-start | bytes 12292
  0.0 13.7 %copy-start.6 = (bf16[1,4,512]{2,1,0:T(4,128)(2,1)S(1)}, bf16[1,4,512]{2,1,0:T(4,128)(2,1)}, u32[]{:S(2)}) copy-start(bf16[1,4,512]{2,1,0:T(4,128)(2,1)} %nk_ref.1) | copy-start | bytes 12292
  0.0 29.0 %collective-permute-start.1 = (bf16[8,256,512]{2,1,0:T(8,128)(2,1)}, bf16[8,256,512]{2,1,0:T(8,128)(2,1)}, u32[]{:S(2)}, u32[]{:S(2)}) collective-permute-start(bf16[8,256,512]{2,1,0:T(8,128)(2,1)} %k0h.1), channel_id=1, source_target_pairs={{0,2},{2,0},{4,6},{6,4},{8,10},{10,8},{12,14},{14,12},{16,18},{18,... | collective-permute-start | bytes 6291464 | tf_op jit(solution)/shard_map/ppermute | solution.py:357
  1.5 27.6 %collective-permute-start.2 = (bf16[8,256,512]{2,1,0:T(8,128)(2,1)}, bf16[8,256,512]{2,1,0:T(8,128)(2,1)}, u32[]{:S(2)}, u32[]{:S(2)}) collective-permute-start(bf16[8,256,512]{2,1,0:T(8,128)(2,1)} %v0h.1), channel_id=1, source_target_pairs={{0,2},{2,0},{4,6},{6,4},{8,10},{10,8},{12,14},{14,12},{16,18},{18,... | collective-permute-start | bytes 6291464 | tf_op jit(solution)/shard_map/ppermute | solution.py:357
  4.3 24.8 %all-to-all-start = ((bf16[32,136,128]{2,1,0:T(8,128)(2,1)}), bf16[32,136,128]{2,1,0:T(8,128)(2,1)S(1)}, u32[]{:S(2)}, u32[]{:S(2)}) async-start(bf16[32,136,128]{2,1,0:T(8,128)(2,1)} %get-tuple-element.15), calls=%async_computation | async-start | bytes 2228224 | tf_op jit(solution)/shard_map/all_to_all | solution.py:351
  12.8 5.2 %collective-permute-start = (bf16[4096,128]{1,0:T(8,128)(2,1)}, bf16[4096,128]{1,0:T(8,128)(2,1)S(1)}, u32[]{:S(2)}, u32[]{:S(2)}) collective-permute-start(bf16[4096,128]{1,0:T(8,128)(2,1)} %w_ref.1), channel_id=1, source_target_pairs={{0,2},{2,0},{4,6},{6,4},{8,10},{10,8},{12,14},{14,12},{16,18},{18,... | collective-permute-start | bytes 3145736 | tf_op jit(solution)/shard_map/ppermute | solution.py:357
  13.7 1.6 %copy-start.1 = (bf16[1,2048,512]{2,1,0:T(8,128)(2,1)S(1)}, bf16[1,2048,512]{2,1,0:T(8,128)(2,1)}, u32[]{:S(2)}) copy-start(bf16[1,2048,512]{2,1,0:T(8,128)(2,1)} %hv_ref.1) | copy-start | bytes 6291460
  18.0 1.0 %copy-start.3 = (bf16[4096,128]{1,0:T(8,128)(2,1)}, bf16[4096,128]{1,0:T(8,128)(2,1)S(1)}, u32[]{:S(2)}) copy-start(bf16[4096,128]{1,0:T(8,128)(2,1)S(1)} %collective-permute-done.x_ref) | copy-start | bytes 3145732
  57.8 20.8 %copy-start.2 = (bf16[4096,128]{1,0:T(8,128)(2,1)S(1)}, bf16[4096,128]{1,0:T(8,128)(2,1)}, u32[]{:S(2)}) copy-start(bf16[4096,128]{1,0:T(8,128)(2,1)} %w_ref.1) | copy-start | bytes 3145732
  57.8 20.8 %copy-start.4 = (bf16[4096,128]{1,0:T(8,128)(2,1)S(1)}, bf16[4096,128]{1,0:T(8,128)(2,1)}, u32[]{:S(2)}) copy-start(bf16[4096,128]{1,0:T(8,128)(2,1)} %copy-done.3) | copy-start | bytes 3145732
  79.2 3.8 %collective-permute-start.3 = (f32[128,128]{1,0:T(8,128)S(1)}, f32[128,128]{1,0:T(8,128)S(1)}, u32[]{:S(2)}, u32[]{:S(2)}) collective-permute-start(f32[128,128]{1,0:T(8,128)S(1)} %get-tuple-element.24), channel_id=1, source_target_pairs={{0,2},{2,0},{4,6},{6,4},{8,10},{10,8},{12,14},{14,12},{16,18},{18,... | collective-permute-start | bytes 196616 | tf_op jit(solution)/shard_map/ppermute | solution.py:357
  83.1 6.9 %collective-permute-start.4 = (f32[256,128]{1,0:T(8,128)S(1)}, f32[256,128]{1,0:T(8,128)S(1)}, u32[]{:S(2)}, u32[]{:S(2)}) collective-permute-start(f32[256,128]{1,0:T(8,128)S(1)} %in_order.1), channel_id=1, source_target_pairs={{0,1},{1,0},{2,3},{3,2},{4,5},{5,4},{6,7},{7,6},{8,9},{9,8},{10,11... | collective-permute-start | bytes 393224 | tf_op jit(solution)/shard_map/ppermute | solution.py:370

commit v5 on v4

--- a/solution.py
+++ b/solution.py
@@ -4,6 +4,7 @@
 from jax.experimental import pallas as pl
 from jax.experimental.pallas import tpu as pltpu
 from jax.sharding import PartitionSpec as P
+
 
 HEAD = 128
 PROMPTS = 8
@@ -15,7 +16,7 @@
 HISTORY = 2048
 KEPT = 1024
 GROUP = 4
-UNROLL = 2
+UNROLL = 4
 PAY = 136
 LOG2E = 1.4426950408889634
 C2 = HEAD ** -0.5 * LOG2E
@@ -46,14 +47,6 @@
 
 def iota(shape, dim):
     return lax.broadcasted_iota(jnp.int32, shape, dim)
-
-
-def spread(tile, out_ref, sem):
-    copies = [pltpu.make_async_copy(tile, out_ref.at[i], sem.at[i]) for i in range(CHIPS)]
-    for copy in copies:
-        copy.start()
-    for copy in copies:
-        copy.wait()
 
 
 def pack_kernel(mem_ref, q_hbm, out_ref, own_ref, q_ref, tmp, tile, sem, in_sem):
@@ -65,9 +58,12 @@
     data = tmp[...].astype(BF)
     own_ref[...] = data
     side = jnp.full((8, HEAD), mem_ref[0, 0], jnp.int32).astype(F32).astype(BF)
-    tile[pl.ds(0, 128), :] = data
-    tile[pl.ds(128, 8), :] = side
-    spread(tile, out_ref, sem)
+    for i in range(CHIPS):
+        tile[i, pl.ds(0, 128), :] = data
+        tile[i, pl.ds(128, 8), :] = side
+    copy = pltpu.make_async_copy(tile, out_ref, sem)
+    copy.start()
+    copy.wait()
 
 
 def pack(membership, queries):
@@ -82,8 +78,8 @@
         scratch_shapes=[
             pltpu.VMEM((1, STEPS, 32 * HEAD), BF),
             pltpu.VMEM((128, HEAD), F32),
-            pltpu.VMEM((PAY, HEAD), BF),
-            pltpu.SemaphoreType.DMA((CHIPS,)),
+            pltpu.VMEM((CHIPS, PAY, HEAD), BF),
+            pltpu.SemaphoreType.DMA(()),
             pltpu.SemaphoreType.DMA(()),
         ],
         compiler_params=LIMIT,

time: 91 us -> 90.5 us (level)
  no operation moved by 1% of the time
where the time goes in v5:
time: 90.5 us; the launch traced here: 90.1 us
  blocking collectives  40.9 us (45%)
  starting transfers between devices  17.2 us (19%)
  waiting for transfers between devices  14.4 us (16%)
  Pallas kernels  13.6 us (15%)
  local copies, waits for them, and re-layouts  2.59 us (3%)
    all_to_all x2, blocking collectives, over_chips(): lax.all_to_all(x, 'req', split_axis=0, concat_axis=0, axis_index_groups=S...  40.9 us
    all_to_all x1, waiting for transfers between devices, over_chips(): lax.all_to_all(x, 'req', split_axis=0, concat_axis=0, axis_index_groups=S...  10 us
    all_to_all x1, starting transfers between devices, over_chips(): lax.all_to_all(x, 'req', split_axis=0, concat_axis=0, axis_index_groups=S...  8.53 us
    pallas_call x1, Pallas kernels, prefix(): pl.pallas_call(prefix_kernel, out_shape=jax.ShapeDtypeStruct((CHIPS, PAY,...  7.28 us
    ppermute x4, starting transfers between devices, swap_cores(): return lax.ppermute(x, 'req', CORE_SWAP)  5.29 us
    ppermute x1, waiting for transfers between devices, local(): theirs = lax.ppermute(part, 'kvh', [(0, 1), (1, 0)])  3.52 us
    ppermute x1, starting transfers between devices, local(): theirs = lax.ppermute(part, 'kvh', [(0, 1), (1, 0)])  3.38 us
    pallas_call x1, Pallas kernels, private(): pl.pallas_call(private_kernel, out_shape=[jax.ShapeDtypeStruct((4, ROWS,...  2.75 us
  transfers between devices with their start and end apart: 6, of which 3 were waited for; matrix products, arithmetic and copies ran while one was open for 0% of the time, Pallas kernels for 5%

profile of v5, /device:TPU:1, one launch (start us, length us, event | category | flops | bytes accessed | tf_op | source)
XLA Modules:
  0.0 90.1 jit_solution(15156822969116306098)
XLA Ops:
  0.0 0.0 copy-start.5
  0.0 0.0 copy-start.6
  0.0 1.4 %collective-permute-start.1 = (bf16[8,256,512]{2,1,0:T(8,128)(2,1)}, bf16[8,256,512]{2,1,0:T(8,128)(2,1)}, u32[]{:S(2)}, u32[]{:S(2)}) collective-permute-start(bf16[8,256,512]{2,1,0:T(8,128)(2,1)} %k0h.1), channel_id=1, source_target_pairs={{0,2},{2,0},{4,6},{6,4},{8,10},{10,8},{12,14},{14,12},{16,18},{18,... | collective-permute-start | bytes 6291464 | tf_op jit(solution)/shard_map/ppermute | solution.py:353
  1.5 0.1 collective-permute-start.2
  2.2 1.8 %pack.1 = (bf16[32,136,128]{2,1,0:T(8,128)(2,1)}, bf16[128,128]{1,0:T(8,128)(2,1)S(1)}) custom-call(s32[1,1]{1,0:T(1,128)S(6)} %copy.11.mem_ref, bf16[1,4,4096]{2,1,0:T(4,128)(2,1)} %q_hbm.1), custom_call_target="tpu_custom_call" | custom-call | tf_op jit(solution)/shard_map/pack/pallas_call | solution.py:70
  4.1 8.5 %all-to-all-start = ((bf16[32,136,128]{2,1,0:T(8,128)(2,1)}), bf16[32,136,128]{2,1,0:T(8,128)(2,1)S(1)}, u32[]{:S(2)}, u32[]{:S(2)}) async-start(bf16[32,136,128]{2,1,0:T(8,128)(2,1)} %get-tuple-element.15), calls=%async_computation | async-start | bytes 2228224 | tf_op jit(solution)/shard_map/all_to_all | solution.py:347
  12.6 0.8 collective-permute-start
  13.5 0.0 copy-done.5
  13.5 0.0 copy-done
  13.5 0.0 copy-done.7
  13.5 0.0 copy-done.6
  13.5 0.0 copy-start.1
  13.5 1.6 %copy-done.1 = bf16[1,2048,512]{2,1,0:T(8,128)(2,1)S(1)} copy-done((bf16[1,2048,512]{2,1,0:T(8,128)(2,1)S(1)}, bf16[1,2048,512]{2,1,0:T(8,128)(2,1)}, u32[]{:S(2)}) %copy-start.1) | copy-done | bytes 2097176
  15.1 2.7 %private.1 = (f32[4,32,128]{2,1,0:T(8,128)S(1)}, f32[4,32,128]{2,1,0:T(8,128)S(1)}) custom-call(bf16[128,128]{1,0:T(8,128)(2,1)S(1)} %get-tuple-element.16.q_ref, s32[1,4,1024]{2,1,0:T(4,128)S(1)} %copy-done.5, bf16[1,2048,512]{2,1,0:T(8,128)(2,1)S(1)} %copy-done, bf16[1,2048,512]{2,1,0:T(8,128)(2,1)S(1)} %copy-done.1, bf16[1,4,512]{2,1,0:T(4,128)(2,1)S(1)} %copy-done.6, ...), custom_call_target="tpu_custom_call" | custom-call | flops 400000000 | bytes 5000000 | tf_op jit(solution)/shard_map/private/pallas_call | solution.py:129
  17.8 0.0 collective-permute-done.x_ref
  17.8 0.0 copy-start.3
  17.8 1.0 %copy-done.3 = bf16[4096,128]{1,0:T(8,128)(2,1)} copy-done((bf16[4096,128]{1,0:T(8,128)(2,1)}, bf16[4096,128]{1,0:T(8,128)(2,1)S(1)}, u32[]{:S(2)}) %copy-start.3) | copy-done | bytes 1048600
  18.8 10.0 %all-to-all-done.q = bf16[32,136,128]{2,1,0:T(8,128)(2,1)S(1)} async-done(((bf16[32,136,128]{2,1,0:T(8,128)(2,1)}), bf16[32,136,128]{2,1,0:T(8,128)(2,1)S(1)}, u32[]{:S(2)}, u32[]{:S(2)}) %all-to-all-start) | async-done | bytes 1114144 | tf_op jit(solution)/shard_map/all_to_all | solution.py:347
  28.8 0.0 collective-permute-done.1.k1h
  28.8 0.0 collective-permute-done.2.v1h
  28.8 7.3 %prefix.1 = bf16[32,136,128]{2,1,0:T(8,128)(2,1)S(1)} custom-call(bf16[32,136,128]{2,1,0:T(8,128)(2,1)S(1)} %all-to-all-done.q, bf16[8,256,512]{2,1,0:T(8,128)(2,1)} %k0h.1, bf16[8,256,512]{2,1,0:T(8,128)(2,1)} %v0h.1, bf16[8,256,512]{2,1,0:T(8,128)(2,1)} %collective-permute-done.1.k1h, bf16[8,256,512]{2,1,0:T(8,128)(2,1)} %collective-permute-done.2.v1h), custom_call_target="tpu_custom_call" | custom-call | flops 1200000000 | bytes 10000000 | tf_op jit(solution)/shard_map/prefix/pallas_call | solution.py:231
  36.1 22.0 %all_to_all.15.in_ref = bf16[32,136,128]{2,1,0:T(8,128)(2,1)S(1)} all-to-all(bf16[32,136,128]{2,1,0:T(8,128)(2,1)S(1)} %prefix.1), channel_id=1, replica_groups={{0,4,8,12,16,20,24,28,32,36,40,44,48,52,56,60,64,68,72,76,80,84,88,92,9..., dimensions={0} | all-to-all | bytes 2228224 | tf_op jit(solution)/shard_map/all_to_all | solution.py:347
  58.1 1.0 %combine.1 = bf16[32,8,2048]{2,1,0:T(8,128)(2,1)S(1)} custom-call(bf16[32,136,128]{2,1,0:T(8,128)(2,1)S(1)} %all_to_all.15.in_ref, f32[4,32,128]{2,1,0:T(8,128)S(1)} %get-tuple-element.20.po_ref, f32[4,32,128]{2,1,0:T(8,128)S(1)} %get-tuple-element.21.pl_ref), custom_call_target="tpu_custom_call" | custom-call | tf_op jit(solution)/shard_map/combine/pallas_call | solution.py:280
  59.2 18.9 %all_to_all.16 = bf16[32,8,2048]{2,1,0:T(8,128)(2,1)S(1)} all-to-all(bf16[32,8,2048]{2,1,0:T(8,128)(2,1)S(1)} %combine.1), channel_id=1, replica_groups={{0,4,8,12,16,20,24,28,32,36,40,44,48,52,56,60,64,68,72,76,80,84,88,92,9..., dimensions={0} | all-to-all | bytes 2097152 | tf_op jit(solution)/shard_map/all_to_all | solution.py:347
  78.0 0.0 copy-done.2
  78.0 0.0 copy-done.4
  78.0 0.7 project.1
  78.7 2.9 %collective-permute-start.3 = (f32[128,128]{1,0:T(8,128)S(1)}, f32[128,128]{1,0:T(8,128)S(1)}, u32[]{:S(2)}, u32[]{:S(2)}) collective-permute-start(f32[128,128]{1,0:T(8,128)S(1)} %get-tuple-element.24), channel_id=1, source_target_pairs={{0,2},{2,0},{4,6},{6,4},{8,10},{10,8},{12,14},{14,12},{16,18},{18,... | collective-permute-start | bytes 196616 | tf_op jit(solution)/shard_map/ppermute | solution.py:353
  81.6 0.9 %collective-permute-done.3.other_ref = f32[128,128]{1,0:T(8,128)S(1)} collective-permute-done((f32[128,128]{1,0:T(8,128)S(1)}, f32[128,128]{1,0:T(8,128)S(1)}, u32[]{:S(2)}, u32[]{:S(2)}) %collective-permute-start.3) | collective-permute-done | bytes 65568 | tf_op jit(solution)/shard_map/ppermute | solution.py:353
  82.6 3.4 %collective-permute-start.4 = (f32[256,128]{1,0:T(8,128)S(1)}, f32[256,128]{1,0:T(8,128)S(1)}, u32[]{:S(2)}, u32[]{:S(2)}) collective-permute-start(f32[256,128]{1,0:T(8,128)S(1)} %in_order.1), channel_id=1, source_target_pairs={{0,1},{1,0},{2,3},{3,2},{4,5},{5,4},{6,7},{7,6},{8,9},{9,8},{10,11... | collective-permute-start | bytes 393224 | tf_op jit(solution)/shard_map/ppermute | solution.py:366
  86.0 3.5 %collective-permute-done.4 = f32[256,128]{1,0:T(8,128)S(1)} collective-permute-done((f32[256,128]{1,0:T(8,128)S(1)}, f32[256,128]{1,0:T(8,128)S(1)}, u32[]{:S(2)}, u32[]{:S(2)}) %collective-permute-start.4) | collective-permute-done | bytes 131104 | tf_op jit(solution)/shard_map/ppermute | solution.py:366
  89.5 0.7 add_convert_fusion
  (5 shorter events, 0.0 us)
Async XLA Ops:
  0.0 13.5 %copy-start.5 = (s32[1,4,1024]{2,1,0:T(4,128)S(1)}, s32[1,4,1024]{2,1,0:T(4,128)}, u32[]{:S(2)}) copy-start(s32[1,4,1024]{2,1,0:T(4,128)} %kept_ref.1) | copy-start | bytes 49156
  0.0 13.5 %copy-start = (bf16[1,2048,512]{2,1,0:T(8,128)(2,1)S(1)}, bf16[1,2048,512]{2,1,0:T(8,128)(2,1)}, u32[]{:S(2)}) copy-start(bf16[1,2048,512]{2,1,0:T(8,128)(2,1)} %hk_ref.1) | copy-start | bytes 6291460
  0.0 13.5 %copy-start.7 = (bf16[1,4,512]{2,1,0:T(4,128)(2,1)S(1)}, bf16[1,4,512]{2,1,0:T(4,128)(2,1)}, u32[]{:S(2)}) copy-start(bf16[1,4,512]{2,1,0:T(4,128)(2,1)} %nv_ref.1) | copy-start | bytes 12292
  0.0 13.5 %copy-start.6 = (bf16[1,4,512]{2,1,0:T(4,128)(2,1)S(1)}, bf16[1,4,512]{2,1,0:T(4,128)(2,1)}, u32[]{:S(2)}) copy-start(bf16[1,4,512]{2,1,0:T(4,128)(2,1)} %nk_ref.1) | copy-start | bytes 12292
  0.0 28.8 %collective-permute-start.1 = (bf16[8,256,512]{2,1,0:T(8,128)(2,1)}, bf16[8,256,512]{2,1,0:T(8,128)(2,1)}, u32[]{:S(2)}, u32[]{:S(2)}) collective-permute-start(bf16[8,256,512]{2,1,0:T(8,128)(2,1)} %k0h.1), channel_id=1, source_target_pairs={{0,2},{2,0},{4,6},{6,4},{8,10},{10,8},{12,14},{14,12},{16,18},{18,... | collective-permute-start | bytes 6291464 | tf_op jit(solution)/shard_map/ppermute | solution.py:353
  1.5 27.4 %collective-permute-start.2 = (bf16[8,256,512]{2,1,0:T(8,128)(2,1)}, bf16[8,256,512]{2,1,0:T(8,128)(2,1)}, u32[]{:S(2)}, u32[]{:S(2)}) collective-permute-start(bf16[8,256,512]{2,1,0:T(8,128)(2,1)} %v0h.1), channel_id=1, source_target_pairs={{0,2},{2,0},{4,6},{6,4},{8,10},{10,8},{12,14},{14,12},{16,18},{18,... | collective-permute-start | bytes 6291464 | tf_op jit(solution)/shard_map/ppermute | solution.py:353
  4.1 24.8 %all-to-all-start = ((bf16[32,136,128]{2,1,0:T(8,128)(2,1)}), bf16[32,136,128]{2,1,0:T(8,128)(2,1)S(1)}, u32[]{:S(2)}, u32[]{:S(2)}) async-start(bf16[32,136,128]{2,1,0:T(8,128)(2,1)} %get-tuple-element.15), calls=%async_computation | async-start | bytes 2228224 | tf_op jit(solution)/shard_map/all_to_all | solution.py:347
  12.6 5.2 %collective-permute-start = (bf16[4096,128]{1,0:T(8,128)(2,1)}, bf16[4096,128]{1,0:T(8,128)(2,1)S(1)}, u32[]{:S(2)}, u32[]{:S(2)}) collective-permute-start(bf16[4096,128]{1,0:T(8,128)(2,1)} %w_ref.1), channel_id=1, source_target_pairs={{0,2},{2,0},{4,6},{6,4},{8,10},{10,8},{12,14},{14,12},{16,18},{18,... | collective-permute-start | bytes 3145736 | tf_op jit(solution)/shard_map/ppermute | solution.py:353
  13.5 1.6 %copy-start.1 = (bf16[1,2048,512]{2,1,0:T(8,128)(2,1)S(1)}, bf16[1,2048,512]{2,1,0:T(8,128)(2,1)}, u32[]{:S(2)}) copy-start(bf16[1,2048,512]{2,1,0:T(8,128)(2,1)} %hv_ref.1) | copy-start | bytes 6291460
  17.8 1.0 %copy-start.3 = (bf16[4096,128]{1,0:T(8,128)(2,1)}, bf16[4096,128]{1,0:T(8,128)(2,1)S(1)}, u32[]{:S(2)}) copy-start(bf16[4096,128]{1,0:T(8,128)(2,1)S(1)} %collective-permute-done.x_ref) | copy-start | bytes 3145732
  58.1 19.9 %copy-start.2 = (bf16[4096,128]{1,0:T(8,128)(2,1)S(1)}, bf16[4096,128]{1,0:T(8,128)(2,1)}, u32[]{:S(2)}) copy-start(bf16[4096,128]{1,0:T(8,128)(2,1)} %w_ref.1) | copy-start | bytes 3145732
  58.1 19.9 %copy-start.4 = (bf16[4096,128]{1,0:T(8,128)(2,1)S(1)}, bf16[4096,128]{1,0:T(8,128)(2,1)}, u32[]{:S(2)}) copy-start(bf16[4096,128]{1,0:T(8,128)(2,1)} %copy-done.3) | copy-start | bytes 3145732
  78.7 3.8 %collective-permute-start.3 = (f32[128,128]{1,0:T(8,128)S(1)}, f32[128,128]{1,0:T(8,128)S(1)}, u32[]{:S(2)}, u32[]{:S(2)}) collective-permute-start(f32[128,128]{1,0:T(8,128)S(1)} %get-tuple-element.24), channel_id=1, source_target_pairs={{0,2},{2,0},{4,6},{6,4},{8,10},{10,8},{12,14},{14,12},{16,18},{18,... | collective-permute-start | bytes 196616 | tf_op jit(solution)/shard_map/ppermute | solution.py:353
  82.6 6.9 %collective-permute-start.4 = (f32[256,128]{1,0:T(8,128)S(1)}, f32[256,128]{1,0:T(8,128)S(1)}, u32[]{:S(2)}, u32[]{:S(2)}) collective-permute-start(f32[256,128]{1,0:T(8,128)S(1)} %in_order.1), channel_id=1, source_target_pairs={{0,1},{1,0},{2,3},{3,2},{4,5},{5,4},{6,7},{7,6},{8,9},{9,8},{10,11... | collective-permute-start | bytes 393224 | tf_op jit(solution)/shard_map/ppermute | solution.py:366

commit v6 on v5

--- a/solution.py
+++ b/solution.py
@@ -287,37 +287,33 @@
     )(x, po, pll)
 
 
-def project_kernel(a_ref, w_ref, x_ref, own_ref, other_ref):
-    acc = jnp.zeros((256, 256), F32)
-    top = (iota((256, 256), 0) & 7) < STEPS
+def project_kernel(a_ref, w_ref, out_ref):
+    parts = []
     for half in range(2):
-        part = jnp.zeros((256, 256), F32)
+        part = jnp.zeros((256, 128), F32)
         for i in range(8):
-            rows = pl.ds(half * 2048 + i * 256, 256)
-            w = jnp.concatenate([w_ref[rows, :], x_ref[rows, :]], axis=1)
+            w = w_ref[pl.ds(half * 2048 + i * 256, 256), :]
             part += mm(a_ref[:, pl.ds(i * 256, 256)], w)
-        acc = jnp.where(top, part, acc) if half == 0 else jnp.where(top, acc, part)
-    sub = iota((8, 256), 0)
+        parts.append(part)
+    acc = jnp.where((iota((256, 128), 0) & 7) < STEPS, parts[0], parts[1])
+    sub = iota((8, 128), 0)
     for k in range(16):
         a, b = acc[k * 16 : k * 16 + 8], acc[k * 16 + 8 : k * 16 + 16]
         a, b = a + pltpu.roll(a, STEPS, 0), b + pltpu.roll(b, STEPS, 0)
-        both = jnp.where(sub < STEPS, a, b)
-        own_ref[pl.ds(k * 8, 8), :] = both[:, :128]
-        other_ref[pl.ds(k * 8, 8), :] = both[:, 128:]
-
-
-def project(a, w, x):
+        out_ref[pl.ds(k * 8, 8), :] = jnp.where(sub < STEPS, a, b)
+
+
+def project(a, w):
     return pl.pallas_call(
         project_kernel,
-        out_shape=[jax.ShapeDtypeStruct((128, 128), F32)] * 2,
-        in_specs=[VM] * 3,
-        out_specs=[VM] * 2,
+        out_shape=jax.ShapeDtypeStruct((128, 128), F32),
+        in_specs=[VM] * 2,
+        out_specs=VM,
         compiler_params=LIMIT,
         cost_estimate=pl.CostEstimate(
-            flops=540_000_000, transcendentals=0, bytes_accessed=3_000_000
+            flops=270_000_000, transcendentals=0, bytes_accessed=2_000_000
         ),
-        name="project",
-    )(a, w, x)
+    )(a, w)
 
 
 def order_kernel(own_ref, other_ref, out_ref):
@@ -361,8 +357,9 @@
     q, po, pll, w1 = lax.optimization_barrier((q, po, pll, w1))
     parts = over_chips(prefix(q, pk, pv, pk1, pv1))
     att = over_chips(combine(parts, po, pll))
-    mine, other = project(att.reshape(256, 2048), out_weight, w1)
-    part = in_order(mine, swap_cores(other))
+    att = att.reshape(256, 2048)
+    other = swap_cores(project(att, w1))
+    part = in_order(project(att, out_weight), other)
     theirs = lax.ppermute(part, "kvh", [(0, 1), (1, 0)])
     return (part + theirs).astype(BF).reshape(REQS, STEPS, 128)
 

time: 90.5 us -> 90.6 us (level)
  transfers between devices with their start and end apart: 6 -> 6, of which waited for: 3 -> 3; matrix products, arithmetic and copies ran while one was open for 0% -> 0% of each run, Pallas kernels for 5% -> 6%
where the time goes in v6:
time: 90.6 us; the launch traced here: 90.3 us
  blocking collectives  41 us (45%)
  starting transfers between devices  17.2 us (19%)
  Pallas kernels  14.3 us (16%)
  waiting for transfers between devices  13.7 us (15%)
  local copies, waits for them, and re-layouts  2.61 us (3%)
    all_to_all x2, blocking collectives, over_chips(): lax.all_to_all(x, 'req', split_axis=0, concat_axis=0, axis_index_groups=S...  41 us
    all_to_all x1, waiting for transfers between devices, over_chips(): lax.all_to_all(x, 'req', split_axis=0, concat_axis=0, axis_index_groups=S...  9.99 us
    all_to_all x1, starting transfers between devices, over_chips(): lax.all_to_all(x, 'req', split_axis=0, concat_axis=0, axis_index_groups=S...  8.53 us
    pallas_call x1, Pallas kernels, prefix(): pl.pallas_call(prefix_kernel, out_shape=jax.ShapeDtypeStruct((CHIPS, PAY,...  7.28 us
    ppermute x4, starting transfers between devices, swap_cores(): return lax.ppermute(x, 'req', CORE_SWAP)  5.29 us
    ppermute x1, waiting for transfers between devices, local(): theirs = lax.ppermute(part, 'kvh', [(0, 1), (1, 0)])  3.52 us
    ppermute x1, starting transfers between devices, local(): theirs = lax.ppermute(part, 'kvh', [(0, 1), (1, 0)])  3.38 us
    pallas_call x1, Pallas kernels, private(): pl.pallas_call(private_kernel, out_shape=[jax.ShapeDtypeStruct((4, ROWS,...  2.75 us
  transfers between devices with their start and end apart: 6, of which 3 were waited for; matrix products, arithmetic and copies ran while one was open for 0% of the time, Pallas kernels for 6%

profile of v6, /device:TPU:1, one launch (start us, length us, event | category | flops | bytes accessed | tf_op | source)
XLA Modules:
  0.0 90.3 jit_solution(6465192598954417158)
XLA Ops:
  0.0 0.0 copy-start.6
  0.0 1.4 %collective-permute-start.1 = (bf16[8,256,512]{2,1,0:T(8,128)(2,1)}, bf16[8,256,512]{2,1,0:T(8,128)(2,1)}, u32[]{:S(2)}, u32[]{:S(2)}) collective-permute-start(bf16[8,256,512]{2,1,0:T(8,128)(2,1)} %k0h.1), channel_id=1, source_target_pairs={{0,2},{2,0},{4,6},{6,4},{8,10},{10,8},{12,14},{14,12},{16,18},{18,... | collective-permute-start | bytes 6291464 | tf_op jit(solution)/shard_map/ppermute | solution.py:349
  1.5 0.1 collective-permute-start.2
  2.2 1.9 %pack.1 = (bf16[32,136,128]{2,1,0:T(8,128)(2,1)}, bf16[128,128]{1,0:T(8,128)(2,1)S(1)}) custom-call(s32[1,1]{1,0:T(1,128)S(6)} %copy.11.mem_ref, bf16[1,4,4096]{2,1,0:T(4,128)(2,1)} %q_hbm.1), custom_call_target="tpu_custom_call" | custom-call | tf_op jit(solution)/shard_map/pack/pallas_call | solution.py:70
  4.1 8.5 %all-to-all-start = ((bf16[32,136,128]{2,1,0:T(8,128)(2,1)}), bf16[32,136,128]{2,1,0:T(8,128)(2,1)S(1)}, u32[]{:S(2)}, u32[]{:S(2)}) async-start(bf16[32,136,128]{2,1,0:T(8,128)(2,1)} %get-tuple-element.13), calls=%async_computation | async-start | bytes 2228224 | tf_op jit(solution)/shard_map/all_to_all | solution.py:343
  12.6 0.8 collective-permute-start
  13.5 0.0 copy-done.5
  13.5 0.0 copy-done
  13.5 0.0 copy-done.7
  13.5 0.0 copy-done.6
  13.5 0.0 copy-start.1
  13.5 1.6 %copy-done.1 = bf16[1,2048,512]{2,1,0:T(8,128)(2,1)S(1)} copy-done((bf16[1,2048,512]{2,1,0:T(8,128)(2,1)S(1)}, bf16[1,2048,512]{2,1,0:T(8,128)(2,1)}, u32[]{:S(2)}) %copy-start.1) | copy-done | bytes 2097176
  15.1 2.7 %private.1 = (f32[4,32,128]{2,1,0:T(8,128)S(1)}, f32[4,32,128]{2,1,0:T(8,128)S(1)}) custom-call(bf16[128,128]{1,0:T(8,128)(2,1)S(1)} %get-tuple-element.14.q_ref, s32[1,4,1024]{2,1,0:T(4,128)S(1)} %copy-done.5, bf16[1,2048,512]{2,1,0:T(8,128)(2,1)S(1)} %copy-done, bf16[1,2048,512]{2,1,0:T(8,128)(2,1)S(1)} %copy-done.1, bf16[1,4,512]{2,1,0:T(4,128)(2,1)S(1)} %copy-done.6, ...), custom_call_target="tpu_custom_call" | custom-call | flops 400000000 | bytes 5000000 | tf_op jit(solution)/shard_map/private/pallas_call | solution.py:129
  17.8 0.0 collective-permute-done.w_ref
  17.8 0.0 copy-start.3
  17.8 1.0 %copy-done.3 = bf16[4096,128]{1,0:T(8,128)(2,1)} copy-done((bf16[4096,128]{1,0:T(8,128)(2,1)}, bf16[4096,128]{1,0:T(8,128)(2,1)S(1)}, u32[]{:S(2)}) %copy-start.3) | copy-done | bytes 1048600
  18.8 10.0 %all-to-all-done.q = bf16[32,136,128]{2,1,0:T(8,128)(2,1)S(1)} async-done(((bf16[32,136,128]{2,1,0:T(8,128)(2,1)}), bf16[32,136,128]{2,1,0:T(8,128)(2,1)S(1)}, u32[]{:S(2)}, u32[]{:S(2)}) %all-to-all-start) | async-done | bytes 1114144 | tf_op jit(solution)/shard_map/all_to_all | solution.py:343
  28.8 0.0 collective-permute-done.1.k1h
  28.8 0.0 collective-permute-done.2.v1h
  28.8 7.3 %prefix.1 = bf16[32,136,128]{2,1,0:T(8,128)(2,1)S(1)} custom-call(bf16[32,136,128]{2,1,0:T(8,128)(2,1)S(1)} %all-to-all-done.q, bf16[8,256,512]{2,1,0:T(8,128)(2,1)} %k0h.1, bf16[8,256,512]{2,1,0:T(8,128)(2,1)} %v0h.1, bf16[8,256,512]{2,1,0:T(8,128)(2,1)} %collective-permute-done.1.k1h, bf16[8,256,512]{2,1,0:T(8,128)(2,1)} %collective-permute-done.2.v1h), custom_call_target="tpu_custom_call" | custom-call | flops 1200000000 | bytes 10000000 | tf_op jit(solution)/shard_map/prefix/pallas_call | solution.py:231
  36.1 22.0 %all_to_all.15.in_ref = bf16[32,136,128]{2,1,0:T(8,128)(2,1)S(1)} all-to-all(bf16[32,136,128]{2,1,0:T(8,128)(2,1)S(1)} %prefix.1), channel_id=1, replica_groups={{0,4,8,12,16,20,24,28,32,36,40,44,48,52,56,60,64,68,72,76,80,84,88,92,9..., dimensions={0} | all-to-all | bytes 2228224 | tf_op jit(solution)/shard_map/all_to_all | solution.py:343
  58.1 1.0 %combine.1 = bf16[32,8,2048]{2,1,0:T(8,128)(2,1)S(1)} custom-call(bf16[32,136,128]{2,1,0:T(8,128)(2,1)S(1)} %all_to_all.15.in_ref, f32[4,32,128]{2,1,0:T(8,128)S(1)} %get-tuple-element.18.po_ref, f32[4,32,128]{2,1,0:T(8,128)S(1)} %get-tuple-element.19.pl_ref), custom_call_target="tpu_custom_call" | custom-call | tf_op jit(solution)/shard_map/combine/pallas_call | solution.py:280
  59.2 0.0 copy-start.2
  59.2 19.0 %all_to_all.16 = bf16[32,8,2048]{2,1,0:T(8,128)(2,1)S(1)} all-to-all(bf16[32,8,2048]{2,1,0:T(8,128)(2,1)S(1)} %combine.1), channel_id=1, replica_groups={{0,4,8,12,16,20,24,28,32,36,40,44,48,52,56,60,64,68,72,76,80,84,88,92,9..., dimensions={0} | all-to-all | bytes 2097152 | tf_op jit(solution)/shard_map/all_to_all | solution.py:343
  78.2 0.0 copy-done.4
  78.2 0.7 shard_map.101
  78.9 2.9 %collective-permute-start.3 = (f32[128,128]{1,0:T(8,128)S(1)}, f32[128,128]{1,0:T(8,128)S(1)}, u32[]{:S(2)}, u32[]{:S(2)}) collective-permute-start(f32[128,128]{1,0:T(8,128)S(1)} %shard_map.101), channel_id=1, source_target_pairs={{0,2},{2,0},{4,6},{6,4},{8,10},{10,8},{12,14},{14,12},{16,18},{18,... | collective-permute-start | bytes 196616 | tf_op jit(solution)/shard_map/ppermute | solution.py:349
  81.8 0.7 shard_map.100.own_ref
  82.5 0.2 collective-permute-done.3.other_ref
  82.7 3.4 %collective-permute-start.4 = (f32[256,128]{1,0:T(8,128)S(1)}, f32[256,128]{1,0:T(8,128)S(1)}, u32[]{:S(2)}, u32[]{:S(2)}) collective-permute-start(f32[256,128]{1,0:T(8,128)S(1)} %in_order.1), channel_id=1, source_target_pairs={{0,1},{1,0},{2,3},{3,2},{4,5},{5,4},{6,7},{7,6},{8,9},{9,8},{10,11... | collective-permute-start | bytes 393224 | tf_op jit(solution)/shard_map/ppermute | solution.py:363
  86.1 3.5 %collective-permute-done.4 = f32[256,128]{1,0:T(8,128)S(1)} collective-permute-done((f32[256,128]{1,0:T(8,128)S(1)}, f32[256,128]{1,0:T(8,128)S(1)}, u32[]{:S(2)}, u32[]{:S(2)}) %collective-permute-start.4) | collective-permute-done | bytes 131104 | tf_op jit(solution)/shard_map/ppermute | solution.py:363
  89.6 0.7 add_convert_fusion
  (6 shorter events, 0.0 us)
Async XLA Ops:
  0.0 13.5 %copy-start.5 = (s32[1,4,1024]{2,1,0:T(4,128)S(1)}, s32[1,4,1024]{2,1,0:T(4,128)}, u32[]{:S(2)}) copy-start(s32[1,4,1024]{2,1,0:T(4,128)} %kept_ref.1) | copy-start | bytes 49156
  0.0 13.5 %copy-start = (bf16[1,2048,512]{2,1,0:T(8,128)(2,1)S(1)}, bf16[1,2048,512]{2,1,0:T(8,128)(2,1)}, u32[]{:S(2)}) copy-start(bf16[1,2048,512]{2,1,0:T(8,128)(2,1)} %hk_ref.1) | copy-start | bytes 6291460
  0.0 13.5 %copy-start.7 = (bf16[1,4,512]{2,1,0:T(4,128)(2,1)S(1)}, bf16[1,4,512]{2,1,0:T(4,128)(2,1)}, u32[]{:S(2)}) copy-start(bf16[1,4,512]{2,1,0:T(4,128)(2,1)} %nv_ref.1) | copy-start | bytes 12292
  0.0 13.5 %copy-start.6 = (bf16[1,4,512]{2,1,0:T(4,128)(2,1)S(1)}, bf16[1,4,512]{2,1,0:T(4,128)(2,1)}, u32[]{:S(2)}) copy-start(bf16[1,4,512]{2,1,0:T(4,128)(2,1)} %nk_ref.1) | copy-start | bytes 12292
  0.0 28.8 %collective-permute-start.1 = (bf16[8,256,512]{2,1,0:T(8,128)(2,1)}, bf16[8,256,512]{2,1,0:T(8,128)(2,1)}, u32[]{:S(2)}, u32[]{:S(2)}) collective-permute-start(bf16[8,256,512]{2,1,0:T(8,128)(2,1)} %k0h.1), channel_id=1, source_target_pairs={{0,2},{2,0},{4,6},{6,4},{8,10},{10,8},{12,14},{14,12},{16,18},{18,... | collective-permute-start | bytes 6291464 | tf_op jit(solution)/shard_map/ppermute | solution.py:349
  1.5 27.4 %collective-permute-start.2 = (bf16[8,256,512]{2,1,0:T(8,128)(2,1)}, bf16[8,256,512]{2,1,0:T(8,128)(2,1)}, u32[]{:S(2)}, u32[]{:S(2)}) collective-permute-start(bf16[8,256,512]{2,1,0:T(8,128)(2,1)} %v0h.1), channel_id=1, source_target_pairs={{0,2},{2,0},{4,6},{6,4},{8,10},{10,8},{12,14},{14,12},{16,18},{18,... | collective-permute-start | bytes 6291464 | tf_op jit(solution)/shard_map/ppermute | solution.py:349
  4.1 24.8 %all-to-all-start = ((bf16[32,136,128]{2,1,0:T(8,128)(2,1)}), bf16[32,136,128]{2,1,0:T(8,128)(2,1)S(1)}, u32[]{:S(2)}, u32[]{:S(2)}) async-start(bf16[32,136,128]{2,1,0:T(8,128)(2,1)} %get-tuple-element.13), calls=%async_computation | async-start | bytes 2228224 | tf_op jit(solution)/shard_map/all_to_all | solution.py:343
  12.6 5.2 %collective-permute-start = (bf16[4096,128]{1,0:T(8,128)(2,1)}, bf16[4096,128]{1,0:T(8,128)(2,1)S(1)}, u32[]{:S(2)}, u32[]{:S(2)}) collective-permute-start(bf16[4096,128]{1,0:T(8,128)(2,1)} %w_ref.1), channel_id=1, source_target_pairs={{0,2},{2,0},{4,6},{6,4},{8,10},{10,8},{12,14},{14,12},{16,18},{18,... | collective-permute-start | bytes 3145736 | tf_op jit(solution)/shard_map/ppermute | solution.py:349
  13.5 1.6 %copy-start.1 = (bf16[1,2048,512]{2,1,0:T(8,128)(2,1)S(1)}, bf16[1,2048,512]{2,1,0:T(8,128)(2,1)}, u32[]{:S(2)}) copy-start(bf16[1,2048,512]{2,1,0:T(8,128)(2,1)} %hv_ref.1) | copy-start | bytes 6291460
  17.8 1.0 %copy-start.3 = (bf16[4096,128]{1,0:T(8,128)(2,1)}, bf16[4096,128]{1,0:T(8,128)(2,1)S(1)}, u32[]{:S(2)}) copy-start(bf16[4096,128]{1,0:T(8,128)(2,1)S(1)} %collective-permute-done.w_ref) | copy-start | bytes 3145732
  58.1 20.0 %copy-start.4 = (bf16[4096,128]{1,0:T(8,128)(2,1)S(1)}, bf16[4096,128]{1,0:T(8,128)(2,1)}, u32[]{:S(2)}) copy-start(bf16[4096,128]{1,0:T(8,128)(2,1)} %copy-done.3) | copy-start | bytes 3145732
  59.2 22.6 %copy-start.2 = (bf16[4096,128]{1,0:T(8,128)(2,1)S(1)}, bf16[4096,128]{1,0:T(8,128)(2,1)}, u32[]{:S(2)}) copy-start(bf16[4096,128]{1,0:T(8,128)(2,1)} %w_ref.1) | copy-start | bytes 3145732
  78.9 3.8 %collective-permute-start.3 = (f32[128,128]{1,0:T(8,128)S(1)}, f32[128,128]{1,0:T(8,128)S(1)}, u32[]{:S(2)}, u32[]{:S(2)}) collective-permute-start(f32[128,128]{1,0:T(8,128)S(1)} %shard_map.101), channel_id=1, source_target_pairs={{0,2},{2,0},{4,6},{6,4},{8,10},{10,8},{12,14},{14,12},{16,18},{18,... | collective-permute-start | bytes 196616 | tf_op jit(solution)/shard_map/ppermute | solution.py:349
  82.7 6.9 %collective-permute-start.4 = (f32[256,128]{1,0:T(8,128)S(1)}, f32[256,128]{1,0:T(8,128)S(1)}, u32[]{:S(2)}, u32[]{:S(2)}) collective-permute-start(f32[256,128]{1,0:T(8,128)S(1)} %in_order.1), channel_id=1, source_target_pairs={{0,1},{1,0},{2,3},{3,2},{4,5},{5,4},{6,7},{7,6},{8,9},{9,8},{10,11... | collective-permute-start | bytes 393224 | tf_op jit(solution)/shard_map/ppermute | solution.py:363
